TPU v7x, 256 devices: a whole 4x4x8 slice. The times are simulated.
256 devices in a mesh: blk: 8 (over y, core), sep: 32 (over x, z).
Axes of the slice: x: 4, y: 4, z: 8, core: 2. Of those that a mesh axis runs over, the one named last changes fastest.
Arguments:
- interior_inverse: float32 [8, 32, 1024, 1024], P('blk', 'sep'), as said below
- coupling: float32 [8, 32, 1024, 512], P('blk', 'sep')
- port_matrix: float32 [8, 32, 512, 512], P('blk', 'sep'), as said below
- interior_current: float32 [8, 32, 1024, 128], P('blk', 'sep'), may hold values from -6 to 6
- port_current: float32 [8, 32, 512, 128], P('blk', 'sep'), may hold values from -6 to 6
- port_list: int32 [8, 32, 512], P('blk', 'sep'), may hold values from 0 to 1023, as said below
- spectral_scale: float32 [], replicated, may hold values from 1.5 to 3
Outputs:
- port_voltage: float32 [32, 1024, 128], P('sep', 'blk')
- interior_voltage: float32 [8, 32, 1024, 128], P('blk', 'sep')
Inputs may be any that keep to these rules, and one draw needn't show every extreme that they name: `port_list`: in each block the first 256 entries are distinct, and so are the last ones. Within one separator group, blocks whose b differ by a multiple of 4 name the same sets, and the sets of the first 4 blocks partition the separator's rows, both for the first and for the last halves. `interior_inverse`: symmetric positive definite. Each block's port_matrix minus coupling^T interior_inverse coupling is symmetric positive definite.
All inputs are finite; a program needn't handle non-finite values.
Results may differ from a plain program's by a relative error of at most 0.0001.
Values sent between devices are 32-bit elements; how exact they have to be, the bound alone decides.
No kernel may reach another device: no remote copies, remote signals or barrier semaphores. Data moves between devices by JAX's collectives and lax.ppermute only.
A program may use at most 64 MiB of HBM per device.

v0:
```python
import functools

import jax
import jax.numpy as jnp
from jax import lax
from jax.experimental import pallas as pl
from jax.experimental.pallas import tpu as pltpu
from jax.sharding import PartitionSpec as P

F32 = jnp.float32
BF16 = jnp.bfloat16
HI = lax.Precision.HIGHEST
MID = lax.Precision.HIGH

N_BLK = 8
N_SEP = 32
SETS = 4
HALF = 256
ROWS = 1024
NI = 1024
COLS = 16
EXTRA = 8
WHOLE = pl.BlockSpec(memory_space=pltpu.VMEM)
SCALARS = pl.BlockSpec(memory_space=pltpu.SMEM)
ROOM = pltpu.CompilerParams(vmem_limit_bytes=56 * 2**20)


def shifted(array, axis, by, size):
    return lax.ppermute(array, axis, [(i, (i + by) % size) for i in range(size)])


def kernel_call(body, outs, *args, scalars=0):
    shapes = [jax.ShapeDtypeStruct(shape, dtype) for shape, dtype in outs]
    return pl.pallas_call(
        body,
        out_shape=shapes,
        in_specs=[SCALARS] * scalars + [WHOLE] * (len(args) - scalars),
        out_specs=[WHOLE] * len(shapes),
        compiler_params=ROOM,
    )(*args)


def split2(value):
    high = value.astype(BF16)
    return high, (value - high.astype(F32)).astype(BF16)


def dot32(left, right):
    return jnp.dot(left, right, preferred_element_type=F32)


def moved(value, choice):
    rows = value.shape[0]
    high = value.astype(BF16)
    rest = value - high.astype(F32)
    middle = rest.astype(BF16)
    low = (rest - middle.astype(F32)).astype(BF16)
    parts = dot32(jnp.concatenate([high, middle, low], axis=0), choice)
    return parts[:rows] + parts[rows : 2 * rows] + parts[2 * rows :]


def places_of(source, target):
    column = jnp.broadcast_to(source, (128, ROWS)).T[:, :1]
    at = lax.broadcasted_iota(jnp.int32, (ROWS, 1), 0).astype(F32)
    return jnp.sum(jnp.where(column == target, at, 0.0), axis=0, keepdims=True).astype(jnp.int32)


def taken(value, places):
    rows = value.shape[0]
    out = []
    for j in range(ROWS // 128):
        place = jnp.broadcast_to(places[:, j * 128 : (j + 1) * 128], (rows, 128))
        lane, tile = place & 127, place >> 7
        result = jnp.zeros((rows, 128), F32)
        for k in range(ROWS // 128):
            piece = jnp.take_along_axis(value[:, k * 128 : (k + 1) * 128], lane, axis=1)
            result = jnp.where(tile == k, piece, result)
        out.append(result)
    return jnp.concatenate(out, axis=1)


def apply_sets(vector, high_ref, low_ref, lower_ref, higher_ref):
    for m in range(SETS):
        at = slice(m * HALF, (m + 1) * HALF)
        piece = jnp.concatenate([vector[:, at], vector[:, ROWS + m * HALF : ROWS + (m + 1) * HALF]], axis=1)
        high, low = split2(piece)
        rows = piece.shape[0]
        both = dot32(jnp.concatenate([high, low], axis=0), high_ref[m])
        image = both[:rows] + both[rows:] + dot32(high, low_ref[m])
        lower_ref[:, at] = image[:, :HALF]
        higher_ref[:, at] = image[:, HALF:]


def matrices_kernel(order_ref, *refs):
    packs, diagonal_ref, high_ref, low_ref = refs[:8], refs[8], refs[9], refs[10]
    row = lax.broadcasted_iota(jnp.int32, (HALF, HALF), 0)
    column = lax.broadcasted_iota(jnp.int32, (HALF, HALF), 1)
    for j in range(SETS):
        m = order_ref[j]
        first = order_ref[SETS + j] == 1
        one, two = packs[2 * j][...], packs[2 * j + 1][...]
        across = jnp.where(first, one, two)
        packed = jnp.where(first, two, one)
        turned = packed.T
        lower = jnp.where(row <= column, packed, turned)
        higher = jnp.where(row > column, packed, turned)
        higher = jnp.where(row == column, diagonal_ref[m], higher)
        for a, b, part in ((0, 0, lower), (0, 1, across), (1, 0, across.T), (1, 1, higher)):
            at = (m, slice(a * HALF, (a + 1) * HALF), slice(b * HALF, (b + 1) * HALF))
            high, low = split2(part)
            high_ref[at] = high
            low_ref[at] = low


def initial_kernel(scale_ref, lower_ref, higher_ref, before_ref, after_ref, into_lower_ref, into_higher_ref, rhs_ref, inverse_ref, damped_ref, level_ref):
    for mine_ref, other_ref, into_ref, side in (
        (lower_ref, before_ref, into_lower_ref, 0),
        (higher_ref, after_ref, into_higher_ref, 1),
    ):
        places = places_of(other_ref[COLS + 1 : COLS + 2], mine_ref[COLS + 1 : COLS + 2])
        into_ref[...] = places
        total = mine_ref[...] + taken(other_ref[...], places)
        at = slice(side * ROWS, (side + 1) * ROWS)
        inverse = 1.0 / total[COLS : COLS + 1]
        rhs_ref[:, at] = total[:COLS]
        inverse_ref[:, at] = inverse
        damped_ref[:, at] = inverse * (1.0 / scale_ref[0])
        level_ref[:, at] = total[:COLS] * inverse


def assembled(lower_ref, higher_ref, before_ref, after_ref, into_lower_ref, into_higher_ref):
    return jnp.concatenate(
        [
            lower_ref[...] + taken(before_ref[...], into_lower_ref[...]),
            higher_ref[...] + taken(after_ref[...], into_higher_ref[...]),
        ],
        axis=1,
    )


def first_kernel(high_ref, low_ref, level_ref, lower_ref, higher_ref):
    apply_sets(level_ref[...], high_ref, low_ref, lower_ref, higher_ref)


def middle_kernel(high_ref, low_ref, into_lower, into_higher, mine_lower, mine_higher, before, after, damped_ref, level_ref, lower_ref, higher_ref, next_ref, sum_ref):
    image = assembled(mine_lower, mine_higher, before, after, into_lower, into_higher)
    level = level_ref[...] - image * damped_ref[...]
    next_ref[...] = level
    sum_ref[...] = level_ref[...] + level
    apply_sets(level, high_ref, low_ref, lower_ref, higher_ref)


def last_kernel(high_ref, low_ref, into_lower, into_higher, mine_lower, mine_higher, before, after, damped_ref, level_ref, total_ref, lower_ref, higher_ref, result_ref):
    image = assembled(mine_lower, mine_higher, before, after, into_lower, into_higher)
    result = total_ref[...] + (level_ref[...] - image * damped_ref[...])
    result_ref[...] = result
    apply_sets(result, high_ref, low_ref, lower_ref, higher_ref)


def image_kernel(high_ref, low_ref, into_lower, into_higher, mine_lower, mine_higher, before, after, inverse_ref, lower_ref, higher_ref, image_ref, level_ref):
    image = assembled(mine_lower, mine_higher, before, after, into_lower, into_higher)
    image_ref[...] = image
    level = image * inverse_ref[...]
    level_ref[...] = level
    apply_sets(level, high_ref, low_ref, lower_ref, higher_ref)


def two_sum(a, b):
    total = a + b
    part = total - a
    return total, (a - (total - part)) + (b - part)


def halves_of(a):
    scaled = a * 4097.0
    high = scaled - (scaled - a)
    return high, a - high


def two_product(a, b):
    product = a * b
    a_high, a_low = halves_of(a)
    b_high, b_low = halves_of(b)
    return product, ((a_high * b_high - product) + a_high * b_low + a_low * b_high) + a_low * b_low


def double_add(a, b):
    total, rest = two_sum(a[0], b[0])
    return two_sum(total, rest + (a[1] + b[1]))


def double_scaled(a, factor):
    total, rest = two_product(a[0], factor)
    return two_sum(total, rest + a[1] * factor)


def inner_product(left, right):
    total = jnp.zeros((COLS, 128), F32)
    rest = jnp.zeros((COLS, 128), F32)
    for k in range(left.shape[1] // 128):
        at = slice(k * 128, (k + 1) * 128)
        product, lost = two_product(left[:, at], right[:, at])
        total, also = two_sum(total, product)
        rest = rest + (lost + also)
    return total, rest


def inner_products(pairs, out_ref):
    results = [inner_product(left, right) for left, right in pairs]
    total = jnp.concatenate([result[0] for result in results], axis=0).T
    rest = jnp.concatenate([result[1] for result in results], axis=0).T
    rows = 64
    while rows >= 8:
        total, lost = two_sum(total[:rows], total[rows:])
        rest = (rest[:rows] + rest[rows:]) + lost
        rows //= 2
    for by in (4, 2, 1):
        total, lost = two_sum(total, pltpu.roll(total, by, 0))
        rest = (rest + pltpu.roll(rest, by, 0)) + lost
    row = lax.broadcasted_iota(jnp.int32, (8, 128), 0)
    message = jnp.where(row == 0, total, jnp.where(row == 1, rest, 0.0))
    for k in range(N_SEP):
        out_ref[k] = message


def closing_kernel(high_ref, low_ref, into_lower, into_higher, mine_lower, mine_higher, before, after, damped_ref, level_ref, total_ref, rhs_ref, search_ref, image_ref, q_lower, q_higher, result_ref, out_ref, w_lower, w_higher):
    image = assembled(mine_lower, mine_higher, before, after, into_lower, into_higher)
    result = total_ref[...] + (level_ref[...] - image * damped_ref[...])
    result_ref[...] = result
    apply_sets(result, high_ref, low_ref, w_lower, w_higher)
    q = jnp.concatenate([q_lower[...], q_higher[...]], axis=1)
    w = jnp.concatenate([w_lower[...], w_higher[...]], axis=1)
    search = search_ref[...]
    rhs, image = rhs_ref[:, :ROWS], image_ref[:, :ROWS]
    own_search, own_result = search[:, :ROWS], result[:, :ROWS]
    inner_products(
        [
            (rhs, own_search),
            (rhs, own_result),
            (image, own_search),
            (image, own_result),
            (search, q),
            (search, w),
            (result, q),
            (result, w),
        ],
        out_ref,
    )


def voltage_kernel(sums_ref, search_ref, turned_ref, names_ref, out_ref):
    total = sums_ref[0]
    rest = jnp.zeros((8, 128), F32)
    for k in range(1, N_SEP):
        total, lost = two_sum(total, sums_ref[k])
        rest = rest + lost
    rest = rest[0:1] + total[1:2]
    columns = [jnp.broadcast_to(line, (128, 128)).T[:, :1] for line in (total[0:1], rest)]
    rz, ru, qz, qu, zq, zw, uq, uw = [
        two_sum(*(column[k * COLS : (k + 1) * COLS] for column in columns)) for k in range(8)
    ]
    alpha = rz[0] / zq[0]
    newer = double_add(
        double_add(rz, double_scaled(double_add(ru, qz), -alpha)), double_scaled(double_scaled(qu, alpha), alpha)
    )[0]
    late_late = double_add(
        double_add(zq, double_scaled(double_add(zw, uq), -alpha)), double_scaled(double_scaled(uw, alpha), alpha)
    )[0]
    late_early = double_add(zq, double_scaled(uq, -alpha))[0]
    early_late = double_add(zq, double_scaled(zw, -alpha))[0]
    beta = newer / rz[0]
    energy = late_late + beta * (late_early + early_late) + beta * beta * zq[0]
    late = newer / energy
    search = search_ref[...]
    value = (alpha + late * beta) * search + late * (search - alpha * turned_ref[...])
    natural = lax.broadcasted_iota(jnp.int32, (1, ROWS), 1).astype(F32)
    rows = taken(value[:, :ROWS], places_of(names_ref[...], natural))
    for b in range(N_BLK):
        m = b % SETS
        out_ref[b, :, :HALF] = value[:, m * HALF : (m + 1) * HALF]
        out_ref[b, :, HALF : 2 * HALF] = value[:, ROWS + m * HALF : ROWS + (m + 1) * HALF]
        out_ref[b, :, 2 * HALF :] = rows[:, b * 128 : (b + 1) * 128]


def sort_kernel(early_ref, ports_ref, schur_ref, outer_ref, product_ref, keep_ref, send_ref, message_ref, low_order_ref, high_order_ref):
    row = lax.broadcasted_iota(jnp.int32, (HALF, HALF), 0)
    column = lax.broadcasted_iota(jnp.int32, (HALF, HALF), 1)
    reduced = outer_ref[...].T - product_ref[...]
    into, moved_sides = [], []
    for side, order_ref in ((0, low_order_ref), (1, high_order_ref)):
        at = slice(side * HALF, (side + 1) * HALF)
        names = ports_ref[:, at].astype(F32)
        across = jnp.broadcast_to(names, (HALF, HALF))
        rank = jnp.sum((across.T < across).astype(F32), axis=0, keepdims=True)
        order = (row.astype(F32) == rank).astype(F32)
        order_ref[...] = order.astype(BF16)
        into.append(order.T.astype(BF16))
        moved_sides.append(moved(jnp.concatenate([reduced[:, at], jnp.broadcast_to(names, (8, HALF))], axis=0), into[side]))
    lower = moved(moved(schur_ref[:HALF, :HALF], into[0]).T, into[0])
    higher = moved(moved(schur_ref[HALF:, HALF:], into[1]).T, into[1])
    across = moved(moved(schur_ref[HALF:, :HALF], into[0]).T, into[1])
    packed = jnp.where(row <= column, lower, higher)
    early = early_ref[0] == 1
    keep_ref[...] = jnp.where(early, across, packed)
    send_ref[...] = jnp.where(early, packed, across)
    extra_row = lax.broadcasted_iota(jnp.int32, (EXTRA, HALF), 0)
    for side, matrix in ((0, lower), (1, higher)):
        at = slice(side * HALF, (side + 1) * HALF)
        diagonal = jnp.sum(jnp.where(row == column, matrix, 0.0), axis=0, keepdims=True)
        names = moved_sides[side][128:]
        extra = jnp.where(extra_row == 0, diagonal, jnp.where(extra_row == 1, names, 0.0))
        for c in range(N_BLK):
            message_ref[c, :COLS, at] = moved_sides[side][c * COLS : (c + 1) * COLS]
            message_ref[c, COLS:, at] = extra


def split_kernel(value_ref, high_ref, low_ref):
    high_ref[...], low_ref[...] = split2(value_ref[...])


def interior_kernel(voltage_ref, low_order_ref, high_order_ref, high_ref, low_ref, inner_ref, interior_ref, port_ref):
    local = jnp.concatenate(
        [moved(voltage_ref[:, :HALF], low_order_ref[...]), moved(voltage_ref[:, HALF : 2 * HALF], high_order_ref[...])],
        axis=1,
    )
    high, low = split2(local)

    def turned(left, right):
        return lax.dot_general(left, right, (((1,), (1,)), ((), ())), preferred_element_type=F32)

    solved = high_ref[...]
    interior_ref[...] = inner_ref[...] - (turned(solved, high) + (turned(solved, low) + turned(low_ref[...], high)))
    port_ref[...] = voltage_ref[:, 2 * HALF :].T


def body(interior_inverse, coupling, port_matrix, interior_current, port_current, port_list, spectral_scale):
    ginv = interior_inverse[0, 0]
    aip = coupling[0, 0]
    app = port_matrix[0, 0]
    inner = interior_current[0, 0]
    outer = port_current[0, 0]
    ports = port_list[0, 0]
    b = lax.axis_index("blk")

    solved = jnp.dot(ginv, aip, precision=MID)
    schur = app - jnp.dot(aip.T, solved, precision=MID)
    product = jnp.dot(inner.T, solved, precision=MID)
    own_inner = jnp.dot(ginv, inner, precision=MID)

    square = ((HALF, HALF), F32)
    order = ((HALF, HALF), BF16)
    keep, send, message, low_order, high_order = kernel_call(
        sort_kernel,
        [square, square, ((N_BLK, COLS + EXTRA, 2 * HALF), F32), order, order],
        (b < SETS).astype(jnp.int32).reshape(1),
        ports.reshape(1, 2 * HALF),
        schur,
        outer,
        product,
        scalars=1,
    )
    mine = keep + shifted(send, "blk", SETS, N_BLK)
    packs = [mine] + [shifted(mine, "blk", d, N_BLK) for d in (4, 2, 6)]
    packs = packs + [lax.ppermute(pack, "blk", [(i, i ^ 1) for i in range(N_BLK)]) for pack in packs]
    sources = [b, (b - 2) % N_BLK, b ^ 1, ((b ^ 1) - 2) % N_BLK]

    parts = lax.all_to_all(message, "blk", 0, 0, tiled=True)
    sums = parts[:SETS] + parts[SETS:]
    by_rows = jnp.transpose(sums, (1, 0, 2))
    lower = by_rows[:, :, :HALF].reshape(COLS + EXTRA, ROWS)
    higher = by_rows[:, :, HALF:].reshape(COLS + EXTRA, ROWS)
    before = shifted(higher, "sep", 1, N_SEP)
    after = shifted(lower, "sep", -1, N_SEP)
    solved_high, solved_low = kernel_call(split_kernel, [((NI, 2 * HALF), BF16)] * 2, solved)
    before, after, own_inner, solved_high, solved_low = lax.optimization_barrier(
        (before, after, own_inner, solved_high, solved_low)
    )
    vec = ((COLS, 2 * ROWS), F32)
    line = ((1, 2 * ROWS), F32)
    side = ((COLS, ROWS), F32)
    choice = ((1, ROWS), jnp.int32)
    into_lower, into_higher, rhs, inverse, damped, level = kernel_call(
        initial_kernel, [choice, choice, vec, line, line, vec], spectral_scale.reshape(1), lower, higher, before, after, scalars=1
    )
    order = jnp.stack([source % SETS for source in sources] + [(source < SETS).astype(jnp.int32) for source in sources])
    matrices = kernel_call(
        matrices_kernel,
        [((SETS, 2 * HALF, 2 * HALF), BF16)] * 2,
        order,
        *packs,
        sums[:, COLS : COLS + 1, HALF:],
        scalars=1,
    )

    def exchanged(low, high):
        return low, high, shifted(high, "sep", 1, N_SEP), shifted(low, "sep", -1, N_SEP)

    def applied(kernel, outs, low, high, *others):
        return kernel_call(kernel, outs, *matrices, into_lower, into_higher, *exchanged(low, high), *others)

    low, high = kernel_call(first_kernel, [side, side], *matrices, level)
    low, high, level, total = applied(middle_kernel, [side, side, vec, vec], low, high, damped, level)
    q_low, q_high, search = applied(last_kernel, [side, side, vec], low, high, damped, level, total)
    low, high, image, level = applied(image_kernel, [side, side, vec, vec], q_low, q_high, inverse)
    low, high, level, total = applied(middle_kernel, [side, side, vec, vec], low, high, damped, level)
    turned, products, _, _ = applied(
        closing_kernel,
        [vec, ((N_SEP, 8, 128), F32), side, side],
        low, high, damped, level, total, rhs, search, image, q_low, q_high,
    )
    products = lax.all_to_all(products, "sep", 0, 0, tiled=True)
    own_names = 0.5 * lower[COLS + 1 : COLS + 2]
    (spread,) = kernel_call(voltage_kernel, [((N_BLK, COLS, 640), F32)], products, search, turned, own_names)
    voltage = lax.all_to_all(spread, "blk", 0, 0, tiled=True).reshape(128, 640)
    interior, port = kernel_call(
        interior_kernel, [((NI, 128), F32), ((128, 128), F32)], voltage, low_order, high_order, solved_high, solved_low, own_inner
    )
    return port[None], interior[None, None]


def solution(mesh):
    return jax.shard_map(
        body,
        mesh=mesh,
        in_specs=(
            P("blk", "sep", None, None),
            P("blk", "sep", None, None),
            P("blk", "sep", None, None),
            P("blk", "sep", None, None),
            P("blk", "sep", None, None),
            P("blk", "sep", None),
            P(),
        ),
        out_specs=(P("sep", "blk", None), P("blk", "sep", None, None)),
        check_vma=False,
    )
```

profile of v0, /device:TPU:1, one launch (start us, length us, event | category | flops | bytes accessed | tf_op | source)
XLA Modules:
  0.0 183.8 jit_solution(320153591013009804)
XLA Ops:
  0.7 1.6 copy-done
  2.2 5.4 %fusion.2.value_ref = f32[1024,512]{1,0:T(8,128)S(1)} fusion(f32[1,1,1024,1024]{3,2,1,0:T(8,128)} %param.7, f32[1,1,1024,512]{3,2,1,0:T(8,128)S(1)} %copy-done), kind=kOutput, calls=%fused_computation.2 | convolution fusion | flops 3221225472 | bytes 8388608 | tf_op jit(solution)/shard_map/dot_general | solution.py:345
  7.7 2.9 %fusion.10.schur_ref = f32[512,512]{1,0:T(8,128)} fusion(f32[1024,512]{1,0:T(8,128)S(1)} %fusion.2.value_ref, f32[1,1,1024,512]{3,2,1,0:T(8,128)S(1)} %copy-done, f32[1,1,512,512]{3,2,1,0:T(8,128)S(1)} %copy-done.4), kind=kOutput, calls=%fused_computation.8 | convolution fusion | flops 1610874880 | bytes 6291456 | tf_op jit(solution)/shard_map/dot_general | solution.py:346
  10.6 1.4 convolution_bitcast_fusion.product_ref
  12.0 3.7 %shard_map.86 = (f32[256,256]{1,0:T(8,128)}, f32[256,256]{1,0:T(8,128)}, f32[8,24,512]{2,1,0:T(8,128)}, bf16[256,256]{1,0:T(8,128)(2,1)}, bf16[256,256]{1,0:T(8,128)(2,1)}) custom-call(s32[1]{0:T(128)} %bitcast.4.early_ref, s32[1,512]{1,0:T(1,128)} %bitcast.58, f32[512,512]{1,0:T(8,128)} %fusion.10.schur_ref, f32[512,128]{1,0:T(8,128)} %bitcast.56, ...), custom_call_target="tpu_custom_call" | custom-call | tf_op jit(solution)/shard_map/pallas_call | solution.py:34
  15.8 6.6 %all-to-all-start = ((f32[8,24,512]{2,1,0:T(8,128)}), f32[8,24,512]{2,1,0:T(8,128)S(1)}, u32[]{:S(2)}, u32[]{:S(2)}) async-start(f32[8,24,512]{2,1,0:T(8,128)} %get-tuple-element.45), calls=%async_computation | async-start | bytes 786432 | tf_op jit(solution)/shard_map/all_to_all | solution.py:367
  22.3 2.9 %collective-permute-start = (f32[256,256]{1,0:T(8,128)}, f32[256,256]{1,0:T(8,128)S(1)}, u32[]{:S(2)}, u32[]{:S(2)}) collective-permute-start(f32[256,256]{1,0:T(8,128)} %get-tuple-element.44), channel_id=1, source_target_pairs={{0,128},{32,160},{64,192},{96,224},{128,0},{160,32},{192,64},{224,... | collective-permute-start | bytes 786440 | tf_op jit(solution)/shard_map/ppermute | solution.py:29
  25.2 10.7 %collective-permute-done = f32[256,256]{1,0:T(8,128)S(1)} collective-permute-done((f32[256,256]{1,0:T(8,128)}, f32[256,256]{1,0:T(8,128)S(1)}, u32[]{:S(2)}, u32[]{:S(2)}) %collective-permute-start) | collective-permute-done | bytes 262176 | tf_op jit(solution)/shard_map/ppermute | solution.py:29
  35.9 1.0 add.33.refs_0_
  36.9 0.5 collective-permute-start.1
  37.4 1.0 collective-permute-start.2
  38.4 1.6 collective-permute-start.3
  40.1 1.5 collective-permute-start.4
  41.6 0.7 slice_bitcast_fusion
  42.3 0.6 copy.16
  42.9 1.0 collective-permute-start.8
  43.9 1.6 collective-permute-done.1.refs_1_
  45.5 3.2 %collective-permute-start.5 = (f32[256,256]{1,0:T(8,128)}, f32[256,256]{1,0:T(8,128)}, u32[]{:S(2)}, u32[]{:S(2)}) collective-permute-start(f32[256,256]{1,0:T(8,128)} %collective-permute-done.1.refs_1_), channel_id=1, source_target_pairs={{0,32},{32,0},{64,96},{96,64},{128,160},{160,128},{192,224},{224,1... | collective-permute-start | bytes 786440 | tf_op jit(solution)/shard_map/ppermute | solution.py:364
  48.8 3.7 %collective-permute-done.2.refs_2_ = f32[256,256]{1,0:T(8,128)} collective-permute-done((f32[256,256]{1,0:T(8,128)S(1)}, f32[256,256]{1,0:T(8,128)}, u32[]{:S(2)}, u32[]{:S(2)}) %collective-permute-start.2) | collective-permute-done | bytes 262176 | tf_op jit(solution)/shard_map/ppermute | solution.py:29
  52.4 0.5 collective-permute-start.6
  52.9 0.0 collective-permute-start.7
  53.0 4.8 %fusion.inner_ref = f32[1024,128]{1,0:T(8,128)} fusion(f32[1,1,1024,1024]{3,2,1,0:T(8,128)} %param.7, f32[1,1,1024,128]{3,2,1,0:T(8,128)S(1)} %copy-done.2), kind=kOutput, calls=%fused_computation | convolution fusion | flops 805306368 | bytes 5242880 | tf_op jit(solution)/shard_map/dot_general | solution.py:348
  57.8 3.1 %shard_map.88 = (bf16[1024,512]{1,0:T(8,128)(2,1)}, bf16[1024,512]{1,0:T(8,128)(2,1)}) custom-call(f32[1024,512]{1,0:T(8,128)} %copy-done.1), custom_call_target="tpu_custom_call" | custom-call | tf_op jit(solution)/shard_map/pallas_call | solution.py:34
  61.6 0.7 stack.50.order_ref
  62.3 7.2 %collective-permute-start.9 = (f32[24,1024]{1,0:T(8,128)S(1)}, f32[24,1024]{1,0:T(8,128)S(1)}, u32[]{:S(2)}, u32[]{:S(2)}) collective-permute-start(f32[24,1024]{1,0:T(8,128)S(1)} %bitcast.54), channel_id=1, source_target_pairs={{0,31},{1,0},{2,1},{3,2},{4,3},{5,4},{6,5},{7,6},{8,7},{9,8},{10,9... | collective-permute-start | bytes 294920 | tf_op jit(solution)/shard_map/ppermute | solution.py:29
  69.5 0.6 slice.28.refs_8_
  70.1 1.0 collective-permute-done.9.after_ref
  71.1 0.6 copy-done.8
  71.8 3.4 %shard_map.89 = (s32[1,1024]{1,0:T(1,128)}, s32[1,1024]{1,0:T(1,128)}, f32[16,2048]{1,0:T(8,128)}, f32[1,2048]{1,0:T(1,128)}, f32[1,2048]{1,0:T(1,128)}, /*index=5*/f32[16,2048]{1,0:T(8,128)}) custom-call(f32[1]{0:T(128)} %bitcast.52.scale_ref, f32[24,1024]{1,0:T(8,128)} %bitcast.55, f32[24,1024]{1,0:T(8,128)} %bitcast.25.higher_ref, ...), custom_call_target="tpu_custom_call" | custom-call | tf_op jit(solution)/shard_map/pallas_call | solution.py:34
  75.2 4.3 %shard_map.87 = (bf16[4,512,512]{2,1,0:T(8,128)(2,1)}, bf16[4,512,512]{2,1,0:T(8,128)(2,1)}) custom-call(s32[8]{0:T(128)} %stack.50.order_ref, f32[256,256]{1,0:T(8,128)} %copy-done.3, f32[256,256]{1,0:T(8,128)} %collective-permute-done.1.refs_1_, f32[256,256]{1,0:T(8,128)} %collective-permute-done.2.refs_2_, f32[256,256]{1,0:T(8,128)} %collective-permute-done.3.refs_3_, ...), custom_call_target="tpu_custom_call" | custom-call | tf_op jit(solution)/shard_map/pallas_call | solution.py:34
  79.5 3.6 %shard_map.90 = (f32[16,1024]{1,0:T(8,128)}, f32[16,1024]{1,0:T(8,128)}) custom-call(bf16[4,512,512]{2,1,0:T(8,128)(2,1)} %get-tuple-element.46.high_ref, bf16[4,512,512]{2,1,0:T(8,128)(2,1)} %get-tuple-element.47.low_ref, f32[16,2048]{1,0:T(8,128)} %get-tuple-element.54.level_ref), custom_call_target="tpu_custom_call" | custom-call | tf_op jit(solution)/shard_map/pallas_call | solution.py:34
  83.1 5.5 %collective-permute-start.11 = (f32[16,1024]{1,0:T(8,128)}, f32[16,1024]{1,0:T(8,128)S(1)}, u32[]{:S(2)}, u32[]{:S(2)}) collective-permute-start(f32[16,1024]{1,0:T(8,128)} %get-tuple-element.55.mine_lower), channel_id=1, source_target_pairs={{0,31},{1,0},{2,1},{3,2},{4,3},{5,4},{6,5},{7,6},{8,7},{9,8},{10,9... | collective-permute-start | bytes 196616 | tf_op jit(solution)/shard_map/ppermute | solution.py:29
  88.6 1.9 %collective-permute-done.10.before = f32[16,1024]{1,0:T(8,128)S(1)} collective-permute-done((f32[16,1024]{1,0:T(8,128)}, f32[16,1024]{1,0:T(8,128)S(1)}, u32[]{:S(2)}, u32[]{:S(2)}) %collective-permute-start.10) | collective-permute-done | bytes 65568 | tf_op jit(solution)/shard_map/ppermute | solution.py:29
  90.5 0.6 copy-done.11
  91.1 0.1 copy-done.16
  91.2 3.9 %shard_map.91 = (f32[16,1024]{1,0:T(8,128)}, f32[16,1024]{1,0:T(8,128)}, f32[16,2048]{1,0:T(8,128)}, f32[16,2048]{1,0:T(8,128)}) custom-call(bf16[4,512,512]{2,1,0:T(8,128)(2,1)} %get-tuple-element.46.high_ref, bf16[4,512,512]{2,1,0:T(8,128)(2,1)} %get-tuple-element.47.low_ref, s32[1,1024]{1,0:T(1,128)} %get-tuple-element.52.into_lower, ...), custom_call_target="tpu_custom_call" | custom-call | tf_op jit(solution)/shard_map/pallas_call | solution.py:34
  95.1 4.8 %collective-permute-start.13 = (f32[16,1024]{1,0:T(8,128)}, f32[16,1024]{1,0:T(8,128)S(1)}, u32[]{:S(2)}, u32[]{:S(2)}) collective-permute-start(f32[16,1024]{1,0:T(8,128)} %get-tuple-element.58.mine_lower), channel_id=1, source_target_pairs={{0,31},{1,0},{2,1},{3,2},{4,3},{5,4},{6,5},{7,6},{8,7},{9,8},{10,9... | collective-permute-start | bytes 196616 | tf_op jit(solution)/shard_map/ppermute | solution.py:29
  99.9 1.8 collective-permute-done.12.before
  101.7 0.6 copy-done.12
  102.4 0.0 copy-done.14
  102.4 4.0 %shard_map.92 = (f32[16,1024]{1,0:T(8,128)}, f32[16,1024]{1,0:T(8,128)}, f32[16,2048]{1,0:T(8,128)}) custom-call(bf16[4,512,512]{2,1,0:T(8,128)(2,1)} %get-tuple-element.46.high_ref, bf16[4,512,512]{2,1,0:T(8,128)(2,1)} %get-tuple-element.47.low_ref, s32[1,1024]{1,0:T(1,128)} %get-tuple-element.52.into_lower, s32[1,1024]{1,0:T(1,128)} %get-tuple-element.53.into_higher, ...), custom_call_target="tpu_custom_call" | custom-call | tf_op jit(solution)/shard_map/pallas_call | solution.py:34
  106.3 5.1 %collective-permute-start.15 = (f32[16,1024]{1,0:T(8,128)}, f32[16,1024]{1,0:T(8,128)S(1)}, u32[]{:S(2)}, u32[]{:S(2)}) collective-permute-start(f32[16,1024]{1,0:T(8,128)} %get-tuple-element.62.mine_lower.q_lower), channel_id=1, source_target_pairs={{0,31},{1,0},{2,1},{3,2},{4,3},{5,4},{6,5},{7,6},{8,7},{9,8},{10,9... | collective-permute-start | bytes 196616 | tf_op jit(solution)/shard_map/ppermute | solution.py:29
  111.4 1.6 collective-permute-done.14.before
  113.0 0.0 collective-permute-done.15.after
  113.0 0.6 copy-done.15
  113.6 0.0 copy-done.18
  113.7 3.9 %shard_map.93 = (f32[16,1024]{1,0:T(8,128)}, f32[16,1024]{1,0:T(8,128)}, f32[16,2048]{1,0:T(8,128)}, f32[16,2048]{1,0:T(8,128)}) custom-call(bf16[4,512,512]{2,1,0:T(8,128)(2,1)} %get-tuple-element.46.high_ref, bf16[4,512,512]{2,1,0:T(8,128)(2,1)} %get-tuple-element.47.low_ref, s32[1,1024]{1,0:T(1,128)} %get-tuple-element.52.into_lower, ...), custom_call_target="tpu_custom_call" | custom-call | tf_op jit(solution)/shard_map/pallas_call | solution.py:34
  117.6 5.1 %collective-permute-start.17 = (f32[16,1024]{1,0:T(8,128)}, f32[16,1024]{1,0:T(8,128)S(1)}, u32[]{:S(2)}, u32[]{:S(2)}) collective-permute-start(f32[16,1024]{1,0:T(8,128)} %get-tuple-element.65.mine_lower), channel_id=1, source_target_pairs={{0,31},{1,0},{2,1},{3,2},{4,3},{5,4},{6,5},{7,6},{8,7},{9,8},{10,9... | collective-permute-start | bytes 196616 | tf_op jit(solution)/shard_map/ppermute | solution.py:29
  122.7 1.8 collective-permute-done.16.before
  124.5 0.6 copy-done.13
  125.1 0.0 copy-done.17
  125.1 3.9 %shard_map.94 = (f32[16,1024]{1,0:T(8,128)}, f32[16,1024]{1,0:T(8,128)}, f32[16,2048]{1,0:T(8,128)}, f32[16,2048]{1,0:T(8,128)}) custom-call(bf16[4,512,512]{2,1,0:T(8,128)(2,1)} %get-tuple-element.46.high_ref, bf16[4,512,512]{2,1,0:T(8,128)(2,1)} %get-tuple-element.47.low_ref, s32[1,1024]{1,0:T(1,128)} %get-tuple-element.52.into_lower, ...), custom_call_target="tpu_custom_call" | custom-call | tf_op jit(solution)/shard_map/pallas_call | solution.py:34
  129.0 4.9 %collective-permute-start.19 = (f32[16,1024]{1,0:T(8,128)}, f32[16,1024]{1,0:T(8,128)S(1)}, u32[]{:S(2)}, u32[]{:S(2)}) collective-permute-start(f32[16,1024]{1,0:T(8,128)} %get-tuple-element.68.mine_lower), channel_id=1, source_target_pairs={{0,31},{1,0},{2,1},{3,2},{4,3},{5,4},{6,5},{7,6},{8,7},{9,8},{10,9... | collective-permute-start | bytes 196616 | tf_op jit(solution)/shard_map/ppermute | solution.py:29
  134.0 1.8 collective-permute-done.18.before
  135.7 0.6 copy-done.9
  136.4 0.0 copy-done.10
  136.4 4.4 %shard_map.95 = (f32[16,2048]{1,0:T(8,128)}, f32[32,8,128]{2,1,0:T(8,128)}, f32[16,1024]{1,0:T(8,128)}, f32[16,1024]{1,0:T(8,128)}) custom-call(bf16[4,512,512]{2,1,0:T(8,128)(2,1)} %get-tuple-element.46.high_ref, bf16[4,512,512]{2,1,0:T(8,128)(2,1)} %get-tuple-element.47.low_ref, s32[1,1024]{1,0:T(1,128)} %get-tuple-element.52.into_lower, ...), custom_call_target="tpu_custom_call" | custom-call | tf_op jit(solution)/shard_map/pallas_call | solution.py:34
  140.8 6.5 %all-to-all-start.1 = ((f32[32,8,128]{2,1,0:T(8,128)}), f32[32,8,128]{2,1,0:T(8,128)S(1)}, u32[]{:S(2)}, u32[]{:S(2)}) async-start(f32[32,8,128]{2,1,0:T(8,128)} %get-tuple-element.75), calls=%async_computation.1 | async-start | bytes 262144 | tf_op jit(solution)/shard_map/all_to_all | solution.py:411
  147.3 0.6 slice_multiply_fusion
  147.9 8.6 %all-to-all-done.1.sums_ref = f32[32,8,128]{2,1,0:T(8,128)S(1)} async-done(((f32[32,8,128]{2,1,0:T(8,128)}), f32[32,8,128]{2,1,0:T(8,128)S(1)}, u32[]{:S(2)}, u32[]{:S(2)}) %all-to-all-start.1) | async-done | bytes 131104 | tf_op jit(solution)/shard_map/all_to_all | solution.py:411
  156.5 0.6 copy-done.5
  157.1 2.7 %shard_map.96 = f32[8,16,640]{2,1,0:T(8,128)} custom-call(f32[32,8,128]{2,1,0:T(8,128)} %copy-done.5, f32[16,2048]{1,0:T(8,128)} %get-tuple-element.73.search_ref, f32[16,2048]{1,0:T(8,128)} %get-tuple-element.76.turned_ref, f32[1,1024]{1,0:T(1,128)} %bitcast.57), custom_call_target="tpu_custom_call" | custom-call | tf_op jit(solution)/shard_map/pallas_call | solution.py:34
  159.9 20.0 %all_to_all.15 = f32[8,16,640]{2,1,0:T(8,128)} all-to-all(f32[8,16,640]{2,1,0:T(8,128)} %shard_map.96), channel_id=1, replica_groups=mesh['blk'=8,'sep'=32] {'blk'}, dimensions={0} | all-to-all | bytes 655360 | tf_op jit(solution)/shard_map/all_to_all | solution.py:414
  179.9 3.9 %shard_map.97 = (f32[1024,128]{1,0:T(8,128)}, f32[128,128]{1,0:T(8,128)}) custom-call(f32[128,640]{1,0:T(8,128)} %bitcast.53, bf16[256,256]{1,0:T(8,128)(2,1)} %get-tuple-element.77.low_order_ref, bf16[256,256]{1,0:T(8,128)(2,1)} %get-tuple-element.78.high_order_ref, bf16[1024,512]{1,0:T(8,128)(2,1)} %get-tuple-element.79.high_ref, ...), custom_call_target="tpu_custom_call" | custom-call | tf_op jit(solution)/shard_map/pallas_call | solution.py:34
  (44 shorter events, 0.2 us)
Async XLA Ops:
  0.6 1.6 copy-start
  2.2 5.4 %copy-start.4 = (f32[1,1,512,512]{3,2,1,0:T(8,128)S(1)}, f32[1,1,512,512]{3,2,1,0:T(8,128)}, u32[]{:S(2)}) copy-start(f32[1,1,512,512]{3,2,1,0:T(8,128)} %param.9) | copy-start | bytes 3145732
  7.7 2.9 %copy-start.1 = (f32[1024,512]{1,0:T(8,128)}, f32[1024,512]{1,0:T(8,128)S(1)}, u32[]{:S(2)}) copy-start(f32[1024,512]{1,0:T(8,128)S(1)} %fusion.2.value_ref) | copy-start | bytes 6291460
  7.7 2.9 %copy-start.2 = (f32[1,1,1024,128]{3,2,1,0:T(8,128)S(1)}, f32[1,1,1024,128]{3,2,1,0:T(8,128)}, u32[]{:S(2)}) copy-start(f32[1,1,1024,128]{3,2,1,0:T(8,128)} %param.10) | copy-start | bytes 1572868
  15.8 25.8 %all-to-all-start = ((f32[8,24,512]{2,1,0:T(8,128)}), f32[8,24,512]{2,1,0:T(8,128)S(1)}, u32[]{:S(2)}, u32[]{:S(2)}) async-start(f32[8,24,512]{2,1,0:T(8,128)} %get-tuple-element.45), calls=%async_computation | async-start | bytes 786432 | tf_op jit(solution)/shard_map/all_to_all | solution.py:367
  22.3 13.6 %collective-permute-start = (f32[256,256]{1,0:T(8,128)}, f32[256,256]{1,0:T(8,128)S(1)}, u32[]{:S(2)}, u32[]{:S(2)}) collective-permute-start(f32[256,256]{1,0:T(8,128)} %get-tuple-element.44), channel_id=1, source_target_pairs={{0,128},{32,160},{64,192},{96,224},{128,0},{160,32},{192,64},{224,... | collective-permute-start | bytes 786440 | tf_op jit(solution)/shard_map/ppermute | solution.py:29
  36.9 20.9 %copy-start.3 = (f32[256,256]{1,0:T(8,128)}, f32[256,256]{1,0:T(8,128)S(1)}, u32[]{:S(2)}) copy-start(f32[256,256]{1,0:T(8,128)S(1)} %add.33.refs_0_) | copy-start | bytes 786436
  36.9 8.6 %collective-permute-start.1 = (f32[256,256]{1,0:T(8,128)S(1)}, f32[256,256]{1,0:T(8,128)}, u32[]{:S(2)}, u32[]{:S(2)}) collective-permute-start(f32[256,256]{1,0:T(8,128)S(1)} %add.33.refs_0_), channel_id=1, source_target_pairs={{0,128},{32,160},{64,192},{96,224},{128,0},{160,32},{192,64},{224,... | collective-permute-start | bytes 786440 | tf_op jit(solution)/shard_map/ppermute | solution.py:29
  37.4 15.0 %collective-permute-start.2 = (f32[256,256]{1,0:T(8,128)S(1)}, f32[256,256]{1,0:T(8,128)}, u32[]{:S(2)}, u32[]{:S(2)}) collective-permute-start(f32[256,256]{1,0:T(8,128)S(1)} %add.33.refs_0_), channel_id=1, source_target_pairs={{0,64},{32,96},{64,128},{96,160},{128,192},{160,224},{192,0},{224,... | collective-permute-start | bytes 786440 | tf_op jit(solution)/shard_map/ppermute | solution.py:29
  38.4 14.5 %collective-permute-start.3 = (f32[256,256]{1,0:T(8,128)S(1)}, f32[256,256]{1,0:T(8,128)}, u32[]{:S(2)}, u32[]{:S(2)}) collective-permute-start(f32[256,256]{1,0:T(8,128)S(1)} %add.33.refs_0_), channel_id=1, source_target_pairs={{0,192},{32,224},{64,0},{96,32},{128,64},{160,96},{192,128},{224,1... | collective-permute-start | bytes 786440 | tf_op jit(solution)/shard_map/ppermute | solution.py:29
  40.1 35.1 %collective-permute-start.4 = (f32[256,256]{1,0:T(8,128)S(1)}, f32[256,256]{1,0:T(8,128)}, u32[]{:S(2)}, u32[]{:S(2)}) collective-permute-start(f32[256,256]{1,0:T(8,128)S(1)} %add.33.refs_0_), channel_id=1, source_target_pairs={{0,32},{32,0},{64,96},{96,64},{128,160},{160,128},{192,224},{224,1... | collective-permute-start | bytes 786440 | tf_op jit(solution)/shard_map/ppermute | solution.py:364
  42.9 19.4 %collective-permute-start.8 = (f32[24,1024]{1,0:T(8,128)}, f32[24,1024]{1,0:T(8,128)}, u32[]{:S(2)}, u32[]{:S(2)}) collective-permute-start(f32[24,1024]{1,0:T(8,128)} %bitcast.25.higher_ref), channel_id=1, source_target_pairs={{0,1},{1,2},{2,3},{3,4},{4,5},{5,6},{6,7},{7,8},{8,9},{9,10},{10,1... | collective-permute-start | bytes 294920 | tf_op jit(solution)/shard_map/ppermute | solution.py:29
  45.5 29.6 %collective-permute-start.5 = (f32[256,256]{1,0:T(8,128)}, f32[256,256]{1,0:T(8,128)}, u32[]{:S(2)}, u32[]{:S(2)}) collective-permute-start(f32[256,256]{1,0:T(8,128)} %collective-permute-done.1.refs_1_), channel_id=1, source_target_pairs={{0,32},{32,0},{64,96},{96,64},{128,160},{160,128},{192,224},{224,1... | collective-permute-start | bytes 786440 | tf_op jit(solution)/shard_map/ppermute | solution.py:364
  52.4 22.7 %collective-permute-start.6 = (f32[256,256]{1,0:T(8,128)}, f32[256,256]{1,0:T(8,128)}, u32[]{:S(2)}, u32[]{:S(2)}) collective-permute-start(f32[256,256]{1,0:T(8,128)} %collective-permute-done.2.refs_2_), channel_id=1, source_target_pairs={{0,32},{32,0},{64,96},{96,64},{128,160},{160,128},{192,224},{224,1... | collective-permute-start | bytes 786440 | tf_op jit(solution)/shard_map/ppermute | solution.py:364
  52.9 22.2 %collective-permute-start.7 = (f32[256,256]{1,0:T(8,128)}, f32[256,256]{1,0:T(8,128)}, u32[]{:S(2)}, u32[]{:S(2)}) collective-permute-start(f32[256,256]{1,0:T(8,128)} %collective-permute-done.3.refs_3_), channel_id=1, source_target_pairs={{0,32},{32,0},{64,96},{96,64},{128,160},{160,128},{192,224},{224,1... | collective-permute-start | bytes 786440 | tf_op jit(solution)/shard_map/ppermute | solution.py:364
  57.7 4.5 %copy-start.6 = (f32[4,3,8,256]{3,2,1,0:T(8,128)S(1)}, f32[4,3,8,256]{3,2,1,0:T(8,128)}, u32[]{:S(2)}) copy-start(f32[4,3,8,256]{3,2,1,0:T(8,128)} %get-tuple-element.85) | copy-start | bytes 294916
  62.3 8.9 %copy-start.7 = (f32[4,3,8,256]{3,2,0,1:T(8,128)}, f32[4,3,8,256]{3,2,0,1:T(8,128)S(1)}, u32[]{:S(2)}) copy-start(f32[4,3,8,256]{3,2,0,1:T(8,128)S(1)} %copy.15) | copy-start | bytes 294916
  62.3 8.9 %collective-permute-start.9 = (f32[24,1024]{1,0:T(8,128)S(1)}, f32[24,1024]{1,0:T(8,128)S(1)}, u32[]{:S(2)}, u32[]{:S(2)}) collective-permute-start(f32[24,1024]{1,0:T(8,128)S(1)} %bitcast.54), channel_id=1, source_target_pairs={{0,31},{1,0},{2,1},{3,2},{4,3},{5,4},{6,5},{7,6},{8,7},{9,8},{10,9... | collective-permute-start | bytes 294920 | tf_op jit(solution)/shard_map/ppermute | solution.py:29
  71.1 0.6 copy-start.8
  83.1 7.4 %collective-permute-start.10 = (f32[16,1024]{1,0:T(8,128)}, f32[16,1024]{1,0:T(8,128)S(1)}, u32[]{:S(2)}, u32[]{:S(2)}) collective-permute-start(f32[16,1024]{1,0:T(8,128)} %get-tuple-element.56.mine_higher), channel_id=1, source_target_pairs={{0,1},{1,2},{2,3},{3,4},{4,5},{5,6},{6,7},{7,8},{8,9},{9,10},{10,1... | collective-permute-start | bytes 196616 | tf_op jit(solution)/shard_map/ppermute | solution.py:29
  83.1 7.4 %collective-permute-start.11 = (f32[16,1024]{1,0:T(8,128)}, f32[16,1024]{1,0:T(8,128)S(1)}, u32[]{:S(2)}, u32[]{:S(2)}) collective-permute-start(f32[16,1024]{1,0:T(8,128)} %get-tuple-element.55.mine_lower), channel_id=1, source_target_pairs={{0,31},{1,0},{2,1},{3,2},{4,3},{5,4},{6,5},{7,6},{8,7},{9,8},{10,9... | collective-permute-start | bytes 196616 | tf_op jit(solution)/shard_map/ppermute | solution.py:29
  90.5 0.6 copy-start.11
  90.5 0.7 copy-start.16
  95.1 6.6 %collective-permute-start.12 = (f32[16,1024]{1,0:T(8,128)}, f32[16,1024]{1,0:T(8,128)S(1)}, u32[]{:S(2)}, u32[]{:S(2)}) collective-permute-start(f32[16,1024]{1,0:T(8,128)} %get-tuple-element.59.mine_higher), channel_id=1, source_target_pairs={{0,1},{1,2},{2,3},{3,4},{4,5},{5,6},{6,7},{7,8},{8,9},{9,10},{10,1... | collective-permute-start | bytes 196616 | tf_op jit(solution)/shard_map/ppermute | solution.py:29
  95.1 6.6 %collective-permute-start.13 = (f32[16,1024]{1,0:T(8,128)}, f32[16,1024]{1,0:T(8,128)S(1)}, u32[]{:S(2)}, u32[]{:S(2)}) collective-permute-start(f32[16,1024]{1,0:T(8,128)} %get-tuple-element.58.mine_lower), channel_id=1, source_target_pairs={{0,31},{1,0},{2,1},{3,2},{4,3},{5,4},{6,5},{7,6},{8,7},{9,8},{10,9... | collective-permute-start | bytes 196616 | tf_op jit(solution)/shard_map/ppermute | solution.py:29
  101.7 0.6 copy-start.12
  101.7 0.6 copy-start.14
  106.3 6.7 %collective-permute-start.14 = (f32[16,1024]{1,0:T(8,128)}, f32[16,1024]{1,0:T(8,128)S(1)}, u32[]{:S(2)}, u32[]{:S(2)}) collective-permute-start(f32[16,1024]{1,0:T(8,128)} %get-tuple-element.63.mine_higher.q_higher), channel_id=1, source_target_pairs={{0,1},{1,2},{2,3},{3,4},{4,5},{5,6},{6,7},{7,8},{8,9},{9,10},{10,1... | collective-permute-start | bytes 196616 | tf_op jit(solution)/shard_map/ppermute | solution.py:29
  106.3 6.7 %collective-permute-start.15 = (f32[16,1024]{1,0:T(8,128)}, f32[16,1024]{1,0:T(8,128)S(1)}, u32[]{:S(2)}, u32[]{:S(2)}) collective-permute-start(f32[16,1024]{1,0:T(8,128)} %get-tuple-element.62.mine_lower.q_lower), channel_id=1, source_target_pairs={{0,31},{1,0},{2,1},{3,2},{4,3},{5,4},{6,5},{7,6},{8,7},{9,8},{10,9... | collective-permute-start | bytes 196616 | tf_op jit(solution)/shard_map/ppermute | solution.py:29
  113.0 0.6 copy-start.15
  113.0 0.6 copy-start.18
  117.6 6.9 %collective-permute-start.16 = (f32[16,1024]{1,0:T(8,128)}, f32[16,1024]{1,0:T(8,128)S(1)}, u32[]{:S(2)}, u32[]{:S(2)}) collective-permute-start(f32[16,1024]{1,0:T(8,128)} %get-tuple-element.66.mine_higher), channel_id=1, source_target_pairs={{0,1},{1,2},{2,3},{3,4},{4,5},{5,6},{6,7},{7,8},{8,9},{9,10},{10,1... | collective-permute-start | bytes 196616 | tf_op jit(solution)/shard_map/ppermute | solution.py:29
  117.6 6.9 %collective-permute-start.17 = (f32[16,1024]{1,0:T(8,128)}, f32[16,1024]{1,0:T(8,128)S(1)}, u32[]{:S(2)}, u32[]{:S(2)}) collective-permute-start(f32[16,1024]{1,0:T(8,128)} %get-tuple-element.65.mine_lower), channel_id=1, source_target_pairs={{0,31},{1,0},{2,1},{3,2},{4,3},{5,4},{6,5},{7,6},{8,7},{9,8},{10,9... | collective-permute-start | bytes 196616 | tf_op jit(solution)/shard_map/ppermute | solution.py:29
  124.4 0.6 copy-start.13
  124.5 0.6 copy-start.17
  129.0 6.7 %collective-permute-start.18 = (f32[16,1024]{1,0:T(8,128)}, f32[16,1024]{1,0:T(8,128)S(1)}, u32[]{:S(2)}, u32[]{:S(2)}) collective-permute-start(f32[16,1024]{1,0:T(8,128)} %get-tuple-element.69.mine_higher), channel_id=1, source_target_pairs={{0,1},{1,2},{2,3},{3,4},{4,5},{5,6},{6,7},{7,8},{8,9},{9,10},{10,1... | collective-permute-start | bytes 196616 | tf_op jit(solution)/shard_map/ppermute | solution.py:29
  129.0 6.7 %collective-permute-start.19 = (f32[16,1024]{1,0:T(8,128)}, f32[16,1024]{1,0:T(8,128)S(1)}, u32[]{:S(2)}, u32[]{:S(2)}) collective-permute-start(f32[16,1024]{1,0:T(8,128)} %get-tuple-element.68.mine_lower), channel_id=1, source_target_pairs={{0,31},{1,0},{2,1},{3,2},{4,3},{5,4},{6,5},{7,6},{8,7},{9,8},{10,9... | collective-permute-start | bytes 196616 | tf_op jit(solution)/shard_map/ppermute | solution.py:29
  135.7 0.6 copy-start.9
  135.7 0.6 copy-start.10
  140.8 15.7 %all-to-all-start.1 = ((f32[32,8,128]{2,1,0:T(8,128)}), f32[32,8,128]{2,1,0:T(8,128)S(1)}, u32[]{:S(2)}, u32[]{:S(2)}) async-start(f32[32,8,128]{2,1,0:T(8,128)} %get-tuple-element.75), calls=%async_computation.1 | async-start | bytes 262144 | tf_op jit(solution)/shard_map/all_to_all | solution.py:411
  156.5 0.6 copy-start.5
where the time goes:
time: 184 us
  starting transfers between devices  58 us (32%)
  Pallas kernels  44.9 us (24%)
  waiting for transfers between devices  34.5 us (19%)
  blocking collectives  20 us (11%)
  matrix products  14.5 us (8%)
  local copies, waits for them, and re-layouts  8.71 us (5%)
    pallas_call x12, Pallas kernels, kernel_call(): pl.pallas_call(body, out_shape=shapes, in_specs=[SCALARS] * scalars + [WH...  44.9 us
    ppermute x16, starting transfers between devices, shifted(): lax.ppermute(array, axis, [(i, (i + by) % size) for i in range(size)])  39.7 us
    ppermute x16, waiting for transfers between devices, shifted(): lax.ppermute(array, axis, [(i, (i + by) % size) for i in range(size)])  25.9 us
    all_to_all x1, blocking collectives, body(): voltage = lax.all_to_all(spread, 'blk', 0, 0, tiled=True).reshape(128, 640)  20 us
    all_to_all x1, waiting for transfers between devices, body(): products = lax.all_to_all(products, 'sep', 0, 0, tiled=True)  8.55 us
    unnamed x39, local copies, waits for them, and re-layouts  6.77 us
    all_to_all x1, starting transfers between devices, body(): parts = lax.all_to_all(message, 'blk', 0, 0, tiled=True)  6.56 us
    all_to_all x1, starting transfers between devices, body(): products = lax.all_to_all(products, 'sep', 0, 0, tiled=True)  6.51 us
  transfers between devices with their start and end apart: 22, of which 10 were waited for; matrix products, arithmetic and copies ran while one was open for 5% of the time, Pallas kernels for 4%

commit v1 on v0

--- a/solution.py
+++ b/solution.py
@@ -22,7 +22,7 @@
 EXTRA = 8
 WHOLE = pl.BlockSpec(memory_space=pltpu.VMEM)
 SCALARS = pl.BlockSpec(memory_space=pltpu.SMEM)
-ROOM = pltpu.CompilerParams(vmem_limit_bytes=56 * 2**20)
+ROOM = pltpu.CompilerParams(vmem_limit_bytes=20 * 2**20)
 
 
 def shifted(array, axis, by, size):
@@ -79,20 +79,24 @@
     return jnp.concatenate(out, axis=1)
 
 
+def apply_set(piece, high_matrix, low_matrix):
+    high, low = split2(piece)
+    rows = piece.shape[0]
+    both = dot32(jnp.concatenate([high, low], axis=0), high_matrix)
+    return both[:rows] + both[rows:] + dot32(high, low_matrix)
+
+
 def apply_sets(vector, high_ref, low_ref, lower_ref, higher_ref):
     for m in range(SETS):
         at = slice(m * HALF, (m + 1) * HALF)
         piece = jnp.concatenate([vector[:, at], vector[:, ROWS + m * HALF : ROWS + (m + 1) * HALF]], axis=1)
-        high, low = split2(piece)
-        rows = piece.shape[0]
-        both = dot32(jnp.concatenate([high, low], axis=0), high_ref[m])
-        image = both[:rows] + both[rows:] + dot32(high, low_ref[m])
+        image = apply_set(piece, high_ref[m], low_ref[m])
         lower_ref[:, at] = image[:, :HALF]
         higher_ref[:, at] = image[:, HALF:]
 
 
 def matrices_kernel(order_ref, *refs):
-    packs, diagonal_ref, high_ref, low_ref = refs[:8], refs[8], refs[9], refs[10]
+    packs, (diagonal_ref, level_ref, high_ref, low_ref, lower_ref, higher_ref) = refs[:8], refs[8:]
     row = lax.broadcasted_iota(jnp.int32, (HALF, HALF), 0)
     column = lax.broadcasted_iota(jnp.int32, (HALF, HALF), 1)
     for j in range(SETS):
@@ -110,6 +114,14 @@
             high, low = split2(part)
             high_ref[at] = high
             low_ref[at] = low
+        start = pl.multiple_of(m * HALF, HALF)
+        image = apply_set(
+            jnp.concatenate([level_ref[:, pl.ds(start, HALF)], level_ref[:, pl.ds(ROWS + start, HALF)]], axis=1),
+            high_ref[m],
+            low_ref[m],
+        )
+        lower_ref[:, pl.ds(start, HALF)] = image[:, :HALF]
+        higher_ref[:, pl.ds(start, HALF)] = image[:, HALF:]
 
 
 def initial_kernel(scale_ref, lower_ref, higher_ref, before_ref, after_ref, into_lower_ref, into_higher_ref, rhs_ref, inverse_ref, damped_ref, level_ref):
@@ -136,10 +148,6 @@
         ],
         axis=1,
     )
-
-
-def first_kernel(high_ref, low_ref, level_ref, lower_ref, higher_ref):
-    apply_sets(level_ref[...], high_ref, low_ref, lower_ref, higher_ref)
 
 
 def middle_kernel(high_ref, low_ref, into_lower, into_higher, mine_lower, mine_higher, before, after, damped_ref, level_ref, lower_ref, higher_ref, next_ref, sum_ref):
@@ -359,9 +367,11 @@
         product,
         scalars=1,
     )
-    mine = keep + shifted(send, "blk", SETS, N_BLK)
+    solved_high, solved_low = kernel_call(split_kernel, [((NI, 2 * HALF), BF16)] * 2, solved)
+    got = shifted(send, "blk", SETS, N_BLK)
+    got, own_inner, solved_high, solved_low = lax.optimization_barrier((got, own_inner, solved_high, solved_low))
+    mine = keep + got
     packs = [mine] + [shifted(mine, "blk", d, N_BLK) for d in (4, 2, 6)]
-    packs = packs + [lax.ppermute(pack, "blk", [(i, i ^ 1) for i in range(N_BLK)]) for pack in packs]
     sources = [b, (b - 2) % N_BLK, b ^ 1, ((b ^ 1) - 2) % N_BLK]
 
     parts = lax.all_to_all(message, "blk", 0, 0, tiled=True)
@@ -371,10 +381,8 @@
     higher = by_rows[:, :, HALF:].reshape(COLS + EXTRA, ROWS)
     before = shifted(higher, "sep", 1, N_SEP)
     after = shifted(lower, "sep", -1, N_SEP)
-    solved_high, solved_low = kernel_call(split_kernel, [((NI, 2 * HALF), BF16)] * 2, solved)
-    before, after, own_inner, solved_high, solved_low = lax.optimization_barrier(
-        (before, after, own_inner, solved_high, solved_low)
-    )
+    *packs, before, after = lax.optimization_barrier((*packs, before, after))
+    packs = packs + [lax.ppermute(pack, "blk", [(i, i ^ 1) for i in range(N_BLK)]) for pack in packs]
     vec = ((COLS, 2 * ROWS), F32)
     line = ((1, 2 * ROWS), F32)
     side = ((COLS, ROWS), F32)
@@ -383,12 +391,13 @@
         initial_kernel, [choice, choice, vec, line, line, vec], spectral_scale.reshape(1), lower, higher, before, after, scalars=1
     )
     order = jnp.stack([source % SETS for source in sources] + [(source < SETS).astype(jnp.int32) for source in sources])
-    matrices = kernel_call(
+    *matrices, low, high = kernel_call(
         matrices_kernel,
-        [((SETS, 2 * HALF, 2 * HALF), BF16)] * 2,
+        [((SETS, 2 * HALF, 2 * HALF), BF16)] * 2 + [side, side],
         order,
         *packs,
         sums[:, COLS : COLS + 1, HALF:],
+        level,
         scalars=1,
     )
 
@@ -398,7 +407,6 @@
     def applied(kernel, outs, low, high, *others):
         return kernel_call(kernel, outs, *matrices, into_lower, into_higher, *exchanged(low, high), *others)
 
-    low, high = kernel_call(first_kernel, [side, side], *matrices, level)
     low, high, level, total = applied(middle_kernel, [side, side, vec, vec], low, high, damped, level)
     q_low, q_high, search = applied(last_kernel, [side, side, vec], low, high, damped, level, total)
     low, high, image, level = applied(image_kernel, [side, side, vec, vec], q_low, q_high, inverse)

time: 184 us -> 139 us (0.76)
  Pallas kernels: 44.9 us -> 15 us
  starting transfers between devices: 58 us -> 39.3 us
  waiting for transfers between devices: 34.5 us -> 40.8 us
  blocking collectives: 20 us -> 17.5 us
    pallas_call x12 -> x11, Pallas kernels: 44.9 us -> 15 us  [kernel_call(): pl.pallas_call(body, out_shape=shapes, in_specs=[SCALARS] * scalars + [WH...]
    ppermute x16, starting transfers between devices: 39.7 us -> 24.6 us  [shifted(): lax.ppermute(array, axis, [(i, (i + by) % size) for i in range(size)])]
    ppermute x16, waiting for transfers between devices: 25.9 us -> 32.4 us  [shifted(): lax.ppermute(array, axis, [(i, (i + by) % size) for i in range(size)])]
    all_to_all x1, starting transfers between devices: 6.51 us -> 3.84 us  [body(): products = lax.all_to_all(products, 'sep', 0, 0, tiled=True)]
    all_to_all x1, blocking collectives: 20 us -> 17.5 us  [body(): voltage = lax.all_to_all(spread, 'blk', 0, 0, tiled=True).reshape(128, 640)]
    unnamed x39 -> x37, local copies, waits for them, and re-layouts: 6.77 us -> 8.72 us
  transfers between devices with their start and end apart: 22 -> 22, of which waited for: 10 -> 14; matrix products, arithmetic and copies ran while one was open for 5% -> 6% of each run, Pallas kernels for 4% -> 1%
where the time goes in v1:
time: 139 us
  waiting for transfers between devices  40.8 us (29%)
  starting transfers between devices  39.3 us (28%)
  blocking collectives  17.5 us (13%)
  Pallas kernels  15 us (11%)
  matrix products  12.9 us (9%)
  local copies, waits for them, and re-layouts  8.83 us (6%)
  other arithmetic  2.9 us (2%)
  between operations  1.58 us (1%)
    ppermute x16, waiting for transfers between devices, shifted(): lax.ppermute(array, axis, [(i, (i + by) % size) for i in range(size)])  32.4 us
    ppermute x16, starting transfers between devices, shifted(): lax.ppermute(array, axis, [(i, (i + by) % size) for i in range(size)])  24.6 us
    all_to_all x1, blocking collectives, body(): voltage = lax.all_to_all(spread, 'blk', 0, 0, tiled=True).reshape(128, 640)  17.5 us
    pallas_call x11, Pallas kernels, kernel_call(): pl.pallas_call(body, out_shape=shapes, in_specs=[SCALARS] * scalars + [WH...  15 us
    unnamed x37, local copies, waits for them, and re-layouts  8.72 us
    all_to_all x1, waiting for transfers between devices, body(): products = lax.all_to_all(products, 'sep', 0, 0, tiled=True)  8.37 us
    all_to_all x1, starting transfers between devices, body(): parts = lax.all_to_all(message, 'blk', 0, 0, tiled=True)  7.17 us
    dot_general x1, matrix products, body(): solved = jnp.dot(ginv, aip, precision=MID)  5.39 us
  transfers between devices with their start and end apart: 22, of which 14 were waited for; matrix products, arithmetic and copies ran while one was open for 6% of the time, Pallas kernels for 1%

profile of v1, /device:TPU:1, one launch (start us, length us, event | category | flops | bytes accessed | tf_op | source)
XLA Modules:
  0.0 138.8 jit_solution(5796907223510606064)
XLA Ops:
  0.6 0.0 copy-start
  0.7 1.6 %copy-done = f32[1,1,1024,512]{3,2,1,0:T(8,128)S(1)} copy-done((f32[1,1,1024,512]{3,2,1,0:T(8,128)S(1)}, f32[1,1,1024,512]{3,2,1,0:T(8,128)}, u32[]{:S(2)}) %copy-start) | copy-done | bytes 2097176
  2.2 5.4 %fusion.2.value_ref = f32[1024,512]{1,0:T(8,128)S(1)} fusion(f32[1,1,1024,1024]{3,2,1,0:T(8,128)} %param.7, f32[1,1,1024,512]{3,2,1,0:T(8,128)S(1)} %copy-done), kind=kOutput, calls=%fused_computation.2 | convolution fusion | flops 3221225472 | bytes 8388608 | tf_op jit(solution)/shard_map/dot_general | solution.py:353
  7.7 0.0 copy-start.16
  7.7 0.8 convolution_bitcast_fusion.product_ref
  8.4 1.2 copy-done.16
  9.6 1.9 %fusion.10.schur_ref = f32[512,512]{1,0:T(8,128)S(1)} fusion(f32[1024,512]{1,0:T(8,128)S(1)} %fusion.2.value_ref, f32[1,1,1024,512]{3,2,1,0:T(8,128)S(1)} %copy-done, f32[1,1,512,512]{3,2,1,0:T(8,128)S(1)} %copy-done.16), kind=kOutput, calls=%fused_computation.8 | convolution fusion | flops 1610874880 | bytes 6291456 | tf_op jit(solution)/shard_map/dot_general | solution.py:354
  11.6 2.0 %shard_map.86 = (f32[256,256]{1,0:T(8,128)S(1)}, f32[256,256]{1,0:T(8,128)S(1)}, f32[8,24,512]{2,1,0:T(8,128)}, bf16[256,256]{1,0:T(8,128)(2,1)S(1)}, bf16[256,256]{1,0:T(8,128)(2,1)S(1)}) custom-call(s32[1]{0:T(128)} %bitcast.4.early_ref, s32[1,512]{1,0:T(1,128)S(1)} %bitcast.60, f32[512,512]{1,0:T(8,128)S(1)} %fusion.10.schur_ref, ...), custom_call_target="tpu_custom_call" | custom-call | tf_op jit(solution)/shard_map/pallas_call | solution.py:34
  13.6 7.2 %all-to-all-start = ((f32[8,24,512]{2,1,0:T(8,128)}), f32[8,24,512]{2,1,0:T(8,128)}, u32[]{:S(2)}, u32[]{:S(2)}) async-start(f32[8,24,512]{2,1,0:T(8,128)} %get-tuple-element.53), calls=%async_computation | async-start | bytes 786432 | tf_op jit(solution)/shard_map/all_to_all | solution.py:377
  20.8 2.9 %collective-permute-start = (f32[256,256]{1,0:T(8,128)S(1)}, f32[256,256]{1,0:T(8,128)S(1)}, u32[]{:S(2)}, u32[]{:S(2)}) collective-permute-start(f32[256,256]{1,0:T(8,128)S(1)} %get-tuple-element.49), channel_id=1, source_target_pairs={{0,128},{32,160},{64,192},{96,224},{128,0},{160,32},{192,64},{224,... | collective-permute-start | bytes 786440 | tf_op jit(solution)/shard_map/ppermute | solution.py:29
  23.7 1.6 %copy-done.2 = f32[1024,512]{1,0:T(8,128)S(1)} copy-done((f32[1024,512]{1,0:T(8,128)S(1)}, f32[1024,512]{1,0:T(8,128)}, u32[]{:S(2)}) %copy-start.2) | copy-done | bytes 2097176
  25.3 0.3 shard_map.87
  25.6 4.9 %fusion.inner_ref = f32[1024,128]{1,0:T(8,128)S(1)} fusion(f32[1,1,1024,1024]{3,2,1,0:T(8,128)} %param.7, f32[1,1,1024,128]{3,2,1,0:T(8,128)} %param.10), kind=kOutput, calls=%fused_computation | convolution fusion | flops 805306368 | bytes 5242880 | tf_op jit(solution)/shard_map/dot_general | solution.py:356
  30.5 3.9 %collective-permute-done = f32[256,256]{1,0:T(8,128)S(1)} collective-permute-done((f32[256,256]{1,0:T(8,128)S(1)}, f32[256,256]{1,0:T(8,128)S(1)}, u32[]{:S(2)}, u32[]{:S(2)}) %collective-permute-start) | collective-permute-done | bytes 262176 | tf_op jit(solution)/shard_map/ppermute | solution.py:29
  34.4 1.0 collective-permute-start.3
  35.4 0.6 collective-permute-start.2
  36.0 0.7 collective-permute-start.1
  36.6 1.0 fusion.17
  37.7 0.0 copy-start.17
  37.8 0.5 collective-permute-start.4
  38.2 6.4 %collective-permute-start.5 = (f32[24,1024]{1,0:T(8,128)S(1)}, f32[24,1024]{1,0:T(8,128)S(1)}, u32[]{:S(2)}, u32[]{:S(2)}) collective-permute-start(f32[24,1024]{1,0:T(8,128)S(1)} %bitcast.54), channel_id=1, source_target_pairs={{0,31},{1,0},{2,1},{3,2},{4,3},{5,4},{6,5},{7,6},{8,7},{9,8},{10,9... | collective-permute-start | bytes 294920 | tf_op jit(solution)/shard_map/ppermute | solution.py:29
  44.6 1.7 %collective-permute-done.4.before_ref = f32[24,1024]{1,0:T(8,128)S(1)} collective-permute-done((f32[24,1024]{1,0:T(8,128)S(1)}, f32[24,1024]{1,0:T(8,128)S(1)}, u32[]{:S(2)}, u32[]{:S(2)}) %collective-permute-start.4) | collective-permute-done | bytes 98336 | tf_op jit(solution)/shard_map/ppermute | solution.py:29
  46.4 0.6 copy-done.10
  47.0 0.6 copy-done.12
  47.7 0.2 collective-permute-done.1.refs_1_
  47.8 3.2 %collective-permute-start.6 = (f32[256,256]{1,0:T(8,128)S(1)}, f32[256,256]{1,0:T(8,128)}, u32[]{:S(2)}, u32[]{:S(2)}) collective-permute-start(f32[256,256]{1,0:T(8,128)S(1)} %add.33.refs_0_), channel_id=1, source_target_pairs={{0,32},{32,0},{64,96},{96,64},{128,160},{160,128},{192,224},{224,1... | collective-permute-start | bytes 786440 | tf_op jit(solution)/shard_map/ppermute | solution.py:385
  51.0 0.0 collective-permute-start.7
  51.0 0.5 collective-permute-start.8
  51.5 0.0 collective-permute-start.9
  52.2 0.1 stack.50.order_ref
  52.3 1.1 slice_add_fusion
  53.4 0.9 copy-done.11
  54.3 0.9 copy-done.13
  55.1 1.7 %shard_map.88 = (s32[1,1024]{1,0:T(1,128)S(1)}, s32[1,1024]{1,0:T(1,128)S(1)}, f32[16,2048]{1,0:T(8,128)S(1)}, f32[1,2048]{1,0:T(1,128)S(1)}, f32[1,2048]{1,0:T(1,128)S(1)}, /*index=5*/f32[16,2048]{1,0:T(8,128)S(1)}) custom-call(f32[1]{0:T(128)} %bitcast.52.scale_ref, f32[24,1024]{1,0:T(8,128)S(1)} %bitcast.55, f32[24,1024]{1,0:T(8,128)S(1)} %bitcast.57, ...), custom_call_target="tpu_custom_call" | custom-call | tf_op jit(solution)/shard_map/pallas_call | solution.py:34
  56.9 2.4 %shard_map.89 = (bf16[4,512,512]{2,1,0:T(8,128)(2,1)S(1)}, bf16[4,512,512]{2,1,0:T(8,128)(2,1)S(1)}, f32[16,1024]{1,0:T(8,128)S(1)}, f32[16,1024]{1,0:T(8,128)S(1)}) custom-call(s32[8]{0:T(128)S(1)} %stack.50.order_ref, f32[256,256]{1,0:T(8,128)S(1)} %add.33.refs_0_, f32[256,256]{1,0:T(8,128)} %collective-permute-done.1.refs_1_, ...), custom_call_target="tpu_custom_call" | custom-call | tf_op jit(solution)/shard_map/pallas_call | solution.py:34
  59.3 6.6 %collective-permute-start.11 = (f32[16,1024]{1,0:T(8,128)S(1)}, f32[16,1024]{1,0:T(8,128)S(1)}, u32[]{:S(2)}, u32[]{:S(2)}) collective-permute-start(f32[16,1024]{1,0:T(8,128)S(1)} %get-tuple-element.65.mine_lower), channel_id=1, source_target_pairs={{0,31},{1,0},{2,1},{3,2},{4,3},{5,4},{6,5},{7,6},{8,7},{9,8},{10,9... | collective-permute-start | bytes 196616 | tf_op jit(solution)/shard_map/ppermute | solution.py:29
  65.9 1.3 collective-permute-done.11.after
  67.2 5.1 %collective-permute-done.10.before = f32[16,1024]{1,0:T(8,128)S(1)} collective-permute-done((f32[16,1024]{1,0:T(8,128)S(1)}, f32[16,1024]{1,0:T(8,128)S(1)}, u32[]{:S(2)}, u32[]{:S(2)}) %collective-permute-start.10) | collective-permute-done | bytes 65568 | tf_op jit(solution)/shard_map/ppermute | solution.py:29
  72.3 0.9 shard_map.90
  73.2 0.0 collective-permute-start.13
  73.2 1.5 %collective-permute-start.12 = (f32[16,1024]{1,0:T(8,128)S(1)}, f32[16,1024]{1,0:T(8,128)S(1)}, u32[]{:S(2)}, u32[]{:S(2)}) collective-permute-start(f32[16,1024]{1,0:T(8,128)S(1)} %get-tuple-element.69.mine_higher), channel_id=1, source_target_pairs={{0,1},{1,2},{2,3},{3,4},{4,5},{5,6},{6,7},{7,8},{8,9},{9,10},{10,1... | collective-permute-start | bytes 196616 | tf_op jit(solution)/shard_map/ppermute | solution.py:29
  74.7 1.6 %collective-permute-done.13.after = f32[16,1024]{1,0:T(8,128)S(1)} collective-permute-done((f32[16,1024]{1,0:T(8,128)S(1)}, f32[16,1024]{1,0:T(8,128)S(1)}, u32[]{:S(2)}, u32[]{:S(2)}) %collective-permute-start.13) | collective-permute-done | bytes 65568 | tf_op jit(solution)/shard_map/ppermute | solution.py:29
  76.3 3.4 %collective-permute-done.12.before = f32[16,1024]{1,0:T(8,128)S(1)} collective-permute-done((f32[16,1024]{1,0:T(8,128)S(1)}, f32[16,1024]{1,0:T(8,128)S(1)}, u32[]{:S(2)}, u32[]{:S(2)}) %collective-permute-start.12) | collective-permute-done | bytes 65568 | tf_op jit(solution)/shard_map/ppermute | solution.py:29
  79.7 0.9 shard_map.91
  80.7 1.5 %collective-permute-start.14 = (f32[16,1024]{1,0:T(8,128)S(1)}, f32[16,1024]{1,0:T(8,128)S(1)}, u32[]{:S(2)}, u32[]{:S(2)}) collective-permute-start(f32[16,1024]{1,0:T(8,128)S(1)} %get-tuple-element.73.mine_higher.q_higher), channel_id=1, source_target_pairs={{0,1},{1,2},{2,3},{3,4},{4,5},{5,6},{6,7},{7,8},{8,9},{9,10},{10,1... | collective-permute-start | bytes 196616 | tf_op jit(solution)/shard_map/ppermute | solution.py:29
  82.1 1.6 %collective-permute-done.15.after = f32[16,1024]{1,0:T(8,128)S(1)} collective-permute-done((f32[16,1024]{1,0:T(8,128)S(1)}, f32[16,1024]{1,0:T(8,128)S(1)}, u32[]{:S(2)}, u32[]{:S(2)}) %collective-permute-start.15) | collective-permute-done | bytes 65568 | tf_op jit(solution)/shard_map/ppermute | solution.py:29
  83.8 3.4 %collective-permute-done.14.before = f32[16,1024]{1,0:T(8,128)S(1)} collective-permute-done((f32[16,1024]{1,0:T(8,128)S(1)}, f32[16,1024]{1,0:T(8,128)S(1)}, u32[]{:S(2)}, u32[]{:S(2)}) %collective-permute-start.14) | collective-permute-done | bytes 65568 | tf_op jit(solution)/shard_map/ppermute | solution.py:29
  87.2 0.9 shard_map.92
  88.1 0.2 collective-permute-start.17
  88.3 1.5 %collective-permute-start.16 = (f32[16,1024]{1,0:T(8,128)S(1)}, f32[16,1024]{1,0:T(8,128)S(1)}, u32[]{:S(2)}, u32[]{:S(2)}) collective-permute-start(f32[16,1024]{1,0:T(8,128)S(1)} %get-tuple-element.76.mine_higher), channel_id=1, source_target_pairs={{0,1},{1,2},{2,3},{3,4},{4,5},{5,6},{6,7},{7,8},{8,9},{9,10},{10,1... | collective-permute-start | bytes 196616 | tf_op jit(solution)/shard_map/ppermute | solution.py:29
  89.7 1.6 %collective-permute-done.17.after = f32[16,1024]{1,0:T(8,128)S(1)} collective-permute-done((f32[16,1024]{1,0:T(8,128)S(1)}, f32[16,1024]{1,0:T(8,128)S(1)}, u32[]{:S(2)}, u32[]{:S(2)}) %collective-permute-start.17) | collective-permute-done | bytes 65568 | tf_op jit(solution)/shard_map/ppermute | solution.py:29
  91.4 3.4 %collective-permute-done.16.before = f32[16,1024]{1,0:T(8,128)S(1)} collective-permute-done((f32[16,1024]{1,0:T(8,128)S(1)}, f32[16,1024]{1,0:T(8,128)S(1)}, u32[]{:S(2)}, u32[]{:S(2)}) %collective-permute-start.16) | collective-permute-done | bytes 65568 | tf_op jit(solution)/shard_map/ppermute | solution.py:29
  94.8 0.9 shard_map.93
  95.7 1.5 %collective-permute-start.18 = (f32[16,1024]{1,0:T(8,128)S(1)}, f32[16,1024]{1,0:T(8,128)S(1)}, u32[]{:S(2)}, u32[]{:S(2)}) collective-permute-start(f32[16,1024]{1,0:T(8,128)S(1)} %get-tuple-element.79.mine_higher), channel_id=1, source_target_pairs={{0,1},{1,2},{2,3},{3,4},{4,5},{5,6},{6,7},{7,8},{8,9},{9,10},{10,1... | collective-permute-start | bytes 196616 | tf_op jit(solution)/shard_map/ppermute | solution.py:29
  97.2 1.9 %collective-permute-done.19.after = f32[16,1024]{1,0:T(8,128)S(1)} collective-permute-done((f32[16,1024]{1,0:T(8,128)S(1)}, f32[16,1024]{1,0:T(8,128)S(1)}, u32[]{:S(2)}, u32[]{:S(2)}) %collective-permute-start.19) | collective-permute-done | bytes 65568 | tf_op jit(solution)/shard_map/ppermute | solution.py:29
  99.1 3.1 %collective-permute-done.18.before = f32[16,1024]{1,0:T(8,128)S(1)} collective-permute-done((f32[16,1024]{1,0:T(8,128)S(1)}, f32[16,1024]{1,0:T(8,128)S(1)}, u32[]{:S(2)}, u32[]{:S(2)}) %collective-permute-start.18) | collective-permute-done | bytes 65568 | tf_op jit(solution)/shard_map/ppermute | solution.py:29
  102.2 1.9 %shard_map.94 = (f32[16,2048]{1,0:T(8,128)S(1)}, f32[32,8,128]{2,1,0:T(8,128)}, f32[16,1024]{1,0:T(8,128)}, f32[16,1024]{1,0:T(8,128)}) custom-call(bf16[4,512,512]{2,1,0:T(8,128)(2,1)S(1)} %get-tuple-element.61.high_ref, bf16[4,512,512]{2,1,0:T(8,128)(2,1)S(1)} %get-tuple-element.62.low_ref, s32[1,1024]{1,0:T(1,128)S(1)} %get-tuple-element.63.into_lower, ...), custom_call_target="tpu_custom_call" | custom-call | tf_op jit(solution)/shard_map/pallas_call | solution.py:34
  104.1 3.8 %all-to-all-start.1 = ((f32[32,8,128]{2,1,0:T(8,128)}), f32[32,8,128]{2,1,0:T(8,128)S(1)}, u32[]{:S(2)}, u32[]{:S(2)}) async-start(f32[32,8,128]{2,1,0:T(8,128)} %get-tuple-element.85), calls=%async_computation.1 | async-start | bytes 262144 | tf_op jit(solution)/shard_map/all_to_all | solution.py:419
  108.0 0.8 slice_multiply_fusion
  108.7 8.4 %all-to-all-done.1.sums_ref = f32[32,8,128]{2,1,0:T(8,128)S(1)} async-done(((f32[32,8,128]{2,1,0:T(8,128)}), f32[32,8,128]{2,1,0:T(8,128)S(1)}, u32[]{:S(2)}, u32[]{:S(2)}) %all-to-all-start.1) | async-done | bytes 131104 | tf_op jit(solution)/shard_map/all_to_all | solution.py:419
  117.1 1.0 shard_map.95
  118.1 17.5 %all_to_all.15 = f32[8,16,640]{2,1,0:T(8,128)S(1)} all-to-all(f32[8,16,640]{2,1,0:T(8,128)S(1)} %shard_map.95), channel_id=1, replica_groups=mesh['blk'=8,'sep'=32] {'blk'}, dimensions={0} | all-to-all | bytes 655360 | tf_op jit(solution)/shard_map/all_to_all | solution.py:422
  135.6 1.2 copy-done.6
  136.8 2.0 %shard_map.96 = (f32[1024,128]{1,0:T(8,128)}, f32[128,128]{1,0:T(8,128)}) custom-call(f32[128,640]{1,0:T(8,128)S(1)} %bitcast.53, bf16[256,256]{1,0:T(8,128)(2,1)S(1)} %get-tuple-element.87.low_order_ref, bf16[256,256]{1,0:T(8,128)(2,1)S(1)} %copy-done.9, bf16[1024,512]{1,0:T(8,128)(2,1)S(1)} %copy-done.4, bf16[1024,512]{1,0:T(8,128)(2,1)S(1)} %copy-done.6, ...), custom_call_target="tpu_custom_call" | custom-call | tf_op jit(solution)/shard_map/pallas_call | solution.py:34
  (41 shorter events, 0.1 us)
Async XLA Ops:
  0.6 1.6 %copy-start = (f32[1,1,1024,512]{3,2,1,0:T(8,128)S(1)}, f32[1,1,1024,512]{3,2,1,0:T(8,128)}, u32[]{:S(2)}) copy-start(f32[1,1,1024,512]{3,2,1,0:T(8,128)} %param.8) | copy-start | bytes 6291460
  2.2 5.4 %copy-start.15 = (f32[1,1,1024,128]{3,2,1,0:T(8,128)S(1)}, f32[1,1,1024,128]{3,2,1,0:T(8,128)}, u32[]{:S(2)}) copy-start(f32[1,1,1024,128]{3,2,1,0:T(8,128)} %param.10) | copy-start | bytes 1572868
  7.6 3.9 %copy-start.1 = (f32[1024,512]{1,0:T(8,128)}, f32[1024,512]{1,0:T(8,128)S(1)}, u32[]{:S(2)}) copy-start(f32[1024,512]{1,0:T(8,128)S(1)} %fusion.2.value_ref) | copy-start | bytes 6291460
  7.7 2.0 %copy-start.16 = (f32[1,1,512,512]{3,2,1,0:T(8,128)S(1)}, f32[1,1,512,512]{3,2,1,0:T(8,128)}, u32[]{:S(2)}) copy-start(f32[1,1,512,512]{3,2,1,0:T(8,128)} %param.9) | copy-start | bytes 3145732
  9.6 1.9 %copy-start.7 = (f32[1,1,512,128]{3,2,1,0:T(8,128)S(1)}, f32[1,1,512,128]{3,2,1,0:T(8,128)}, u32[]{:S(2)}) copy-start(f32[1,1,512,128]{3,2,1,0:T(8,128)} %param.11) | copy-start | bytes 786436
  9.6 1.9 %copy-start.14 = (s32[1,1,512]{2,1,0:T(1,128)S(1)}, s32[1,1,512]{2,1,0:T(1,128)}, u32[]{:S(2)}) copy-start(s32[1,1,512]{2,1,0:T(1,128)} %param.12) | copy-start | bytes 6148
  13.6 16.8 %copy-start.8 = (bf16[256,256]{1,0:T(8,128)(2,1)}, bf16[256,256]{1,0:T(8,128)(2,1)S(1)}, u32[]{:S(2)}) copy-start(bf16[256,256]{1,0:T(8,128)(2,1)S(1)} %get-tuple-element.88.high_order_ref) | copy-start | bytes 393220
  13.6 23.0 %all-to-all-start = ((f32[8,24,512]{2,1,0:T(8,128)}), f32[8,24,512]{2,1,0:T(8,128)}, u32[]{:S(2)}, u32[]{:S(2)}) async-start(f32[8,24,512]{2,1,0:T(8,128)} %get-tuple-element.53), calls=%async_computation | async-start | bytes 786432 | tf_op jit(solution)/shard_map/all_to_all | solution.py:377
  20.8 13.6 %collective-permute-start = (f32[256,256]{1,0:T(8,128)S(1)}, f32[256,256]{1,0:T(8,128)S(1)}, u32[]{:S(2)}, u32[]{:S(2)}) collective-permute-start(f32[256,256]{1,0:T(8,128)S(1)} %get-tuple-element.49), channel_id=1, source_target_pairs={{0,128},{32,160},{64,192},{96,224},{128,0},{160,32},{192,64},{224,... | collective-permute-start | bytes 786440 | tf_op jit(solution)/shard_map/ppermute | solution.py:29
  23.7 1.6 %copy-start.2 = (f32[1024,512]{1,0:T(8,128)S(1)}, f32[1024,512]{1,0:T(8,128)}, u32[]{:S(2)}) copy-start(f32[1024,512]{1,0:T(8,128)} %copy-done.1) | copy-start | bytes 6291460
  25.5 4.9 %copy-start.3 = (bf16[1024,512]{1,0:T(8,128)(2,1)}, bf16[1024,512]{1,0:T(8,128)(2,1)S(1)}, u32[]{:S(2)}) copy-start(bf16[1024,512]{1,0:T(8,128)(2,1)S(1)} %get-tuple-element.89.high_ref) | copy-start | bytes 3145732
  25.6 4.9 %copy-start.5 = (bf16[1024,512]{1,0:T(8,128)(2,1)}, bf16[1024,512]{1,0:T(8,128)(2,1)S(1)}, u32[]{:S(2)}) copy-start(bf16[1024,512]{1,0:T(8,128)(2,1)S(1)} %get-tuple-element.90.low_ref) | copy-start | bytes 3145732
  34.4 13.3 %collective-permute-start.3 = (f32[256,256]{1,0:T(8,128)S(1)}, f32[256,256]{1,0:T(8,128)S(1)}, u32[]{:S(2)}, u32[]{:S(2)}) collective-permute-start(f32[256,256]{1,0:T(8,128)S(1)} %add.33.refs_0_), channel_id=1, source_target_pairs={{0,192},{32,224},{64,0},{96,32},{128,64},{160,96},{192,128},{224,1... | collective-permute-start | bytes 786440 | tf_op jit(solution)/shard_map/ppermute | solution.py:29
  35.4 12.3 %collective-permute-start.2 = (f32[256,256]{1,0:T(8,128)S(1)}, f32[256,256]{1,0:T(8,128)}, u32[]{:S(2)}, u32[]{:S(2)}) collective-permute-start(f32[256,256]{1,0:T(8,128)S(1)} %add.33.refs_0_), channel_id=1, source_target_pairs={{0,64},{32,96},{64,128},{96,160},{128,192},{160,224},{192,0},{224,... | collective-permute-start | bytes 786440 | tf_op jit(solution)/shard_map/ppermute | solution.py:29
  36.0 11.9 %collective-permute-start.1 = (f32[256,256]{1,0:T(8,128)S(1)}, f32[256,256]{1,0:T(8,128)}, u32[]{:S(2)}, u32[]{:S(2)}) collective-permute-start(f32[256,256]{1,0:T(8,128)S(1)} %add.33.refs_0_), channel_id=1, source_target_pairs={{0,128},{32,160},{64,192},{96,224},{128,0},{160,32},{192,64},{224,... | collective-permute-start | bytes 786440 | tf_op jit(solution)/shard_map/ppermute | solution.py:29
  37.7 13.3 %copy-start.17 = (f32[24,4,512]{2,0,1:T(8,128)}, f32[24,4,512]{2,0,1:T(8,128)S(1)}, u32[]{:S(2)}) copy-start(f32[24,4,512]{2,0,1:T(8,128)S(1)} %fusion.17) | copy-start | bytes 589828
  37.8 8.6 %collective-permute-start.4 = (f32[24,1024]{1,0:T(8,128)S(1)}, f32[24,1024]{1,0:T(8,128)S(1)}, u32[]{:S(2)}, u32[]{:S(2)}) collective-permute-start(f32[24,1024]{1,0:T(8,128)S(1)} %bitcast.56), channel_id=1, source_target_pairs={{0,1},{1,2},{2,3},{3,4},{4,5},{5,6},{6,7},{7,8},{8,9},{9,10},{10,1... | collective-permute-start | bytes 294920 | tf_op jit(solution)/shard_map/ppermute | solution.py:29
  38.2 8.8 %collective-permute-start.5 = (f32[24,1024]{1,0:T(8,128)S(1)}, f32[24,1024]{1,0:T(8,128)S(1)}, u32[]{:S(2)}, u32[]{:S(2)}) collective-permute-start(f32[24,1024]{1,0:T(8,128)S(1)} %bitcast.54), channel_id=1, source_target_pairs={{0,31},{1,0},{2,1},{3,2},{4,3},{5,4},{6,5},{7,6},{8,7},{9,8},{10,9... | collective-permute-start | bytes 294920 | tf_op jit(solution)/shard_map/ppermute | solution.py:29
  46.4 0.7 copy-start.10
  47.0 0.6 copy-start.12
  47.8 9.0 %collective-permute-start.6 = (f32[256,256]{1,0:T(8,128)S(1)}, f32[256,256]{1,0:T(8,128)}, u32[]{:S(2)}, u32[]{:S(2)}) collective-permute-start(f32[256,256]{1,0:T(8,128)S(1)} %add.33.refs_0_), channel_id=1, source_target_pairs={{0,32},{32,0},{64,96},{96,64},{128,160},{160,128},{192,224},{224,1... | collective-permute-start | bytes 786440 | tf_op jit(solution)/shard_map/ppermute | solution.py:385
  51.0 5.8 %collective-permute-start.7 = (f32[256,256]{1,0:T(8,128)}, f32[256,256]{1,0:T(8,128)}, u32[]{:S(2)}, u32[]{:S(2)}) collective-permute-start(f32[256,256]{1,0:T(8,128)} %collective-permute-done.1.refs_1_), channel_id=1, source_target_pairs={{0,32},{32,0},{64,96},{96,64},{128,160},{160,128},{192,224},{224,1... | collective-permute-start | bytes 786440 | tf_op jit(solution)/shard_map/ppermute | solution.py:385
  51.0 5.8 %collective-permute-start.8 = (f32[256,256]{1,0:T(8,128)}, f32[256,256]{1,0:T(8,128)}, u32[]{:S(2)}, u32[]{:S(2)}) collective-permute-start(f32[256,256]{1,0:T(8,128)} %collective-permute-done.2.refs_2_), channel_id=1, source_target_pairs={{0,32},{32,0},{64,96},{96,64},{128,160},{160,128},{192,224},{224,1... | collective-permute-start | bytes 786440 | tf_op jit(solution)/shard_map/ppermute | solution.py:385
  51.5 5.3 %collective-permute-start.9 = (f32[256,256]{1,0:T(8,128)S(1)}, f32[256,256]{1,0:T(8,128)}, u32[]{:S(2)}, u32[]{:S(2)}) collective-permute-start(f32[256,256]{1,0:T(8,128)S(1)} %collective-permute-done.3.refs_3_), channel_id=1, source_target_pairs={{0,32},{32,0},{64,96},{96,64},{128,160},{160,128},{192,224},{224,1... | collective-permute-start | bytes 786440 | tf_op jit(solution)/shard_map/ppermute | solution.py:385
  53.4 0.9 copy-start.11
  54.3 0.9 copy-start.13
  59.3 7.9 %collective-permute-start.11 = (f32[16,1024]{1,0:T(8,128)S(1)}, f32[16,1024]{1,0:T(8,128)S(1)}, u32[]{:S(2)}, u32[]{:S(2)}) collective-permute-start(f32[16,1024]{1,0:T(8,128)S(1)} %get-tuple-element.65.mine_lower), channel_id=1, source_target_pairs={{0,31},{1,0},{2,1},{3,2},{4,3},{5,4},{6,5},{7,6},{8,7},{9,8},{10,9... | collective-permute-start | bytes 196616 | tf_op jit(solution)/shard_map/ppermute | solution.py:29
  65.9 6.4 %collective-permute-start.10 = (f32[16,1024]{1,0:T(8,128)S(1)}, f32[16,1024]{1,0:T(8,128)S(1)}, u32[]{:S(2)}, u32[]{:S(2)}) collective-permute-start(f32[16,1024]{1,0:T(8,128)S(1)} %get-tuple-element.66.mine_higher), channel_id=1, source_target_pairs={{0,1},{1,2},{2,3},{3,4},{4,5},{5,6},{6,7},{7,8},{8,9},{9,10},{10,1... | collective-permute-start | bytes 196616 | tf_op jit(solution)/shard_map/ppermute | solution.py:29
  73.2 3.1 %collective-permute-start.13 = (f32[16,1024]{1,0:T(8,128)S(1)}, f32[16,1024]{1,0:T(8,128)S(1)}, u32[]{:S(2)}, u32[]{:S(2)}) collective-permute-start(f32[16,1024]{1,0:T(8,128)S(1)} %get-tuple-element.68.mine_lower), channel_id=1, source_target_pairs={{0,31},{1,0},{2,1},{3,2},{4,3},{5,4},{6,5},{7,6},{8,7},{9,8},{10,9... | collective-permute-start | bytes 196616 | tf_op jit(solution)/shard_map/ppermute | solution.py:29
  73.2 6.5 %collective-permute-start.12 = (f32[16,1024]{1,0:T(8,128)S(1)}, f32[16,1024]{1,0:T(8,128)S(1)}, u32[]{:S(2)}, u32[]{:S(2)}) collective-permute-start(f32[16,1024]{1,0:T(8,128)S(1)} %get-tuple-element.69.mine_higher), channel_id=1, source_target_pairs={{0,1},{1,2},{2,3},{3,4},{4,5},{5,6},{6,7},{7,8},{8,9},{9,10},{10,1... | collective-permute-start | bytes 196616 | tf_op jit(solution)/shard_map/ppermute | solution.py:29
  80.6 3.1 %collective-permute-start.15 = (f32[16,1024]{1,0:T(8,128)S(1)}, f32[16,1024]{1,0:T(8,128)S(1)}, u32[]{:S(2)}, u32[]{:S(2)}) collective-permute-start(f32[16,1024]{1,0:T(8,128)S(1)} %get-tuple-element.72.mine_lower.q_lower), channel_id=1, source_target_pairs={{0,31},{1,0},{2,1},{3,2},{4,3},{5,4},{6,5},{7,6},{8,7},{9,8},{10,9... | collective-permute-start | bytes 196616 | tf_op jit(solution)/shard_map/ppermute | solution.py:29
  80.7 6.5 %collective-permute-start.14 = (f32[16,1024]{1,0:T(8,128)S(1)}, f32[16,1024]{1,0:T(8,128)S(1)}, u32[]{:S(2)}, u32[]{:S(2)}) collective-permute-start(f32[16,1024]{1,0:T(8,128)S(1)} %get-tuple-element.73.mine_higher.q_higher), channel_id=1, source_target_pairs={{0,1},{1,2},{2,3},{3,4},{4,5},{5,6},{6,7},{7,8},{8,9},{9,10},{10,1... | collective-permute-start | bytes 196616 | tf_op jit(solution)/shard_map/ppermute | solution.py:29
  88.1 3.3 %collective-permute-start.17 = (f32[16,1024]{1,0:T(8,128)S(1)}, f32[16,1024]{1,0:T(8,128)S(1)}, u32[]{:S(2)}, u32[]{:S(2)}) collective-permute-start(f32[16,1024]{1,0:T(8,128)S(1)} %get-tuple-element.75.mine_lower), channel_id=1, source_target_pairs={{0,31},{1,0},{2,1},{3,2},{4,3},{5,4},{6,5},{7,6},{8,7},{9,8},{10,9... | collective-permute-start | bytes 196616 | tf_op jit(solution)/shard_map/ppermute | solution.py:29
  88.3 6.5 %collective-permute-start.16 = (f32[16,1024]{1,0:T(8,128)S(1)}, f32[16,1024]{1,0:T(8,128)S(1)}, u32[]{:S(2)}, u32[]{:S(2)}) collective-permute-start(f32[16,1024]{1,0:T(8,128)S(1)} %get-tuple-element.76.mine_higher), channel_id=1, source_target_pairs={{0,1},{1,2},{2,3},{3,4},{4,5},{5,6},{6,7},{7,8},{8,9},{9,10},{10,1... | collective-permute-start | bytes 196616 | tf_op jit(solution)/shard_map/ppermute | solution.py:29
  95.7 3.4 %collective-permute-start.19 = (f32[16,1024]{1,0:T(8,128)S(1)}, f32[16,1024]{1,0:T(8,128)S(1)}, u32[]{:S(2)}, u32[]{:S(2)}) collective-permute-start(f32[16,1024]{1,0:T(8,128)S(1)} %get-tuple-element.78.mine_lower), channel_id=1, source_target_pairs={{0,31},{1,0},{2,1},{3,2},{4,3},{5,4},{6,5},{7,6},{8,7},{9,8},{10,9... | collective-permute-start | bytes 196616 | tf_op jit(solution)/shard_map/ppermute | solution.py:29
  95.7 6.5 %collective-permute-start.18 = (f32[16,1024]{1,0:T(8,128)S(1)}, f32[16,1024]{1,0:T(8,128)S(1)}, u32[]{:S(2)}, u32[]{:S(2)}) collective-permute-start(f32[16,1024]{1,0:T(8,128)S(1)} %get-tuple-element.79.mine_higher), channel_id=1, source_target_pairs={{0,1},{1,2},{2,3},{3,4},{4,5},{5,6},{6,7},{7,8},{8,9},{9,10},{10,1... | collective-permute-start | bytes 196616 | tf_op jit(solution)/shard_map/ppermute | solution.py:29
  102.2 33.4 %copy-start.9 = (bf16[256,256]{1,0:T(8,128)(2,1)S(1)}, bf16[256,256]{1,0:T(8,128)(2,1)}, u32[]{:S(2)}) copy-start(bf16[256,256]{1,0:T(8,128)(2,1)} %copy-done.8) | copy-start | bytes 393220
  104.1 13.0 %all-to-all-start.1 = ((f32[32,8,128]{2,1,0:T(8,128)}), f32[32,8,128]{2,1,0:T(8,128)S(1)}, u32[]{:S(2)}, u32[]{:S(2)}) async-start(f32[32,8,128]{2,1,0:T(8,128)} %get-tuple-element.85), calls=%async_computation.1 | async-start | bytes 262144 | tf_op jit(solution)/shard_map/all_to_all | solution.py:419
  117.1 18.5 %copy-start.4 = (bf16[1024,512]{1,0:T(8,128)(2,1)S(1)}, bf16[1024,512]{1,0:T(8,128)(2,1)}, u32[]{:S(2)}) copy-start(bf16[1024,512]{1,0:T(8,128)(2,1)} %copy-done.3) | copy-start | bytes 3145732
  135.6 1.2 copy-start.6
